TPU v7x, 32 devices: a whole 2x2x4 slice. The times are simulated.
32 devices in a mesh: groups: 2 (over x), tm: 16 (over z, y, core).
Axes of the slice: x: 2, y: 2, z: 4, core: 2. Of those that a mesh axis runs over, the one named last changes fastest.
Arguments:
- samples: float32 [16384, 2048], P('groups', 'tm'), parts along dimension 0, may hold values from -6 to 6
- test_matrix: float32 [4096, 256], P(('groups', 'tm')), parts along dimension 0, may hold values from -0.125 to 0.125
Outputs:
- basis: float32 [16384, 256], P(('groups', 'tm')), parts along dimension 0
- coordinates: float32 [512, 2048], P('groups', 'tm'), parts along dimension 0
There are 2 independent parts, one for each index of `groups`. A program takes and returns all parts, laid end to end along the dimension named above; each array names one. Nothing has to cross between parts.
All inputs are finite; a program needn't handle non-finite values.
Results may differ from a plain program's by a relative error of at most 0.0003.
Values sent between devices are 32-bit elements; how exact they have to be, the bound alone decides.
No kernel may reach another device: no remote copies, remote signals or barrier semaphores. Data moves between devices by JAX's collectives and lax.ppermute only.
A program may use at most 64 MiB of HBM per device.

v0:
```python
import jax
import jax.numpy as jnp
from jax import lax
from jax.sharding import PartitionSpec as P


def local_gram(rows):
    return jnp.dot(
        rows.T, rows, precision=lax.Precision.HIGHEST, preferred_element_type=jnp.float32
    )


def local(samples, test_matrix):
    highest = lax.Precision.HIGHEST
    channels = samples.shape[0]
    sample_rows = samples
    sketch = lax.psum_scatter(
        jnp.dot(sample_rows, test_matrix, precision=highest, preferred_element_type=jnp.float32),
        "tm",
        scatter_dimension=0,
        tiled=True,
    )
    sample_rows = samples
    projected = jnp.einsum(
        "rk,rs->ks",
        lax.all_gather(sketch, "tm", axis=0, tiled=True),
        sample_rows,
        precision=highest,
    )
    gram_one = lax.psum(local_gram(sketch), "tm")
    factor_one = jnp.linalg.cholesky(gram_one)
    orthonormal = jax.scipy.linalg.solve_triangular(factor_one, sketch.T, lower=True).T
    coordinates = jax.scipy.linalg.solve_triangular(factor_one, projected, lower=True)
    return (orthonormal * float(channels) ** 0.5, coordinates)


def solution(mesh):
    placed = (P("groups", "tm"), P(("groups", "tm"), None))
    return jax.shard_map(
        local,
        mesh=mesh,
        in_specs=placed,
        out_specs=(P(("groups", "tm"), None), P("groups", "tm")),
        check_vma=False,
    )
```

profile of v0, /device:TPU:0, one launch (start us, length us, event | category | flops | bytes accessed | tf_op | source)
XLA Modules:
  0.0 319.4 jit_solution(12343590044157621184)
XLA Ops:
  7.2 0.0 copy-start
  7.2 0.0 reduce-scatter.2.cloned.1.call-start
  7.2 0.8 copy-done
  8.1 10.4 %fusion.14 = f32[8192,256]{1,0:T(8,128)} fusion(f32[8192,128]{1,0:T(8,128)} %param.2, f32[128,256]{1,0:T(8,128)S(1)} %copy-done), kind=kOutput, calls=%fused_computation.36 | convolution fusion | flops 3221225472 | bytes 12713984 | tf_op jit(solution)/shard_map/dot_general | solution.py:18
  18.5 0.0 reduce-scatter.2.cloned.1.call-update
  18.5 0.0 all-reduce.3.cloned.1.call-start
  18.5 106.3 %reduce-scatter.2.cloned.1.call-done = f32[512,256]{1,0:T(8,128)} async-done(((f32[8192,256]{1,0:T(8,128)}), f32[512,256]{1,0:T(8,128)}) %reduce-scatter.2.cloned.1.call-update) | async-done | bytes 524304 | tf_op jit(solution)/shard_map/reduce_scatter | solution.py:17
  124.8 0.0 copy-start.1
  124.8 3.0 fusion.15
  127.8 0.0 all-reduce.3.cloned.1.call-update
  127.8 0.2 all-gather.2.cloned.1.call-start
  128.0 0.5 all-gather.2.cloned.1.call-update
  128.6 89.7 %all-reduce.3.cloned.1.call-done = f32[256,256]{0,1:T(8,128)} async-done(((f32[256,256]{0,1:T(8,128)}), f32[256,256]{0,1:T(8,128)}) %all-reduce.3.cloned.1.call-update) | async-done | bytes 262160 | tf_op jit(solution)/shard_map/psum | solution.py:30
  218.2 1.1 copy.5
  219.3 1.0 fusion.3
  220.3 11.7 %cholesky.50 = f32[128,128]{1,0:T(8,128)S(1)} custom-call(f32[128,128]{1,0:T(8,128)S(1)} %cholesky.118), custom_call_target="Cholesky" | custom-call | tf_op jit(solution)/shard_map/jit(cholesky)/cholesky | solution.py:31
  232.1 9.8 %custom-call.18 = f32[1,128,128]{1,2,0:T(8,128)S(1)} custom-call(f32[1,128,128]{2,1,0:T(8,128)S(1)} %get-tuple-element.25), custom_call_target="InvertDiagBlocksLowerTriangular" | custom-call | tf_op jit(solution)/shard_map/jit(cholesky)/cholesky | solution.py:31
  241.9 0.2 constant_dynamic-update-slice_fusion.1
  242.1 0.3 convolution_subtract_fusion.2
  242.4 11.7 %cholesky.105 = f32[128,128]{1,0:T(8,128)S(1)} custom-call(f32[128,128]{1,0:T(8,128)S(1)} %convolution_subtract_fusion.2), custom_call_target="Cholesky" | custom-call | tf_op jit(solution)/shard_map/jit(cholesky)/cholesky | solution.py:31
  254.1 0.7 compare_reduce_fusion
  256.1 0.1 triangular_solve.72
  256.2 4.1 %while.1 = (s32[]{:T(128)}, f32[256,256]{1,0:T(8,128)S(1)}, s32[2,2]{1,0:T(2,128)S(1)}, f32[2,128,128]{2,1,0:T(8,128)S(1)}, s32[]{:T(128)}) while((s32[]{:T(128)}, f32[256,256]{1,0:T(8,128)S(1)}, s32[2,2]{1,0:T(2,128)S(1)}, f32[2,128,128]{2,1,0:T(8,128)S(1)}, s32[]{:T(128)}) %tuple.28), condition=%wide.while_cond, body=%wide.while_body.sunk | while | flops 2 | bytes 131189 | solution.py:32
  256.4 0.6 fusion.30
  257.0 1.4 bitcast_dynamic-update-slice_fusion.2
  258.4 0.6 fusion.30
  259.0 1.4 bitcast_dynamic-update-slice_fusion.2
  260.4 19.7 %custom-call.19 = f32[2,128,128]{1,2,0:T(8,128)S(1)} custom-call(f32[2,128,128]{2,1,0:T(8,128)S(1)} %get-tuple-element.9), custom_call_target="InvertDiagBlocksLowerTriangular" | custom-call | tf_op jit(solution)/shard_map/jit(_solve_triangular)/triangular_solve | solution.py:32
  280.0 0.0 copy-done.1
  280.1 0.4 fusion.1
  280.5 0.6 convolution_subtract_fusion
  281.1 0.4 fusion.10
  281.5 0.1 fusion
  281.6 1.0 copy.6
  282.6 12.7 %all-gather.2.cloned.1.call-done = f32[8192,256]{1,0:T(8,128)} async-done(((f32[512,256]{1,0:T(8,128)}), f32[8192,256]{1,0:T(8,128)}) %all-gather.2.cloned.1.call-update) | async-done | bytes 8388624 | tf_op jit(solution)/shard_map/all_gather | solution.py:26
  295.2 16.2 %fusion.16 = f32[256,128]{1,0:T(8,128)S(1)} fusion(f32[8192,256]{1,0:T(8,128)} %all-gather.2.cloned.1.call-done, f32[8192,128]{1,0:T(8,128)} %param.2), kind=kOutput, calls=%fused_computation.38 | convolution fusion | flops 3221225472 | bytes 12713984 | tf_op jit(solution)/shard_map/rk,rs->ks/dot_general | solution.py:24
  311.5 0.3 fusion.4
  311.7 0.2 convolution_subtract_fusion.1
  312.0 0.3 fusion.9
  312.2 0.7 pad_maximum_fusion
  (9 shorter events, 0.1 us)
Async XLA Ops:
  7.2 0.9 copy-start
  7.2 117.6 %reduce-scatter.2.cloned.1.call-start = ((), (), s32[]{:S(2)}) async-start(), calls=%async_computation.1 | async-start | bytes 8912896 | tf_op jit(solution)/shard_map/reduce_scatter | solution.py:17
  18.5 199.7 %all-reduce.3.cloned.1.call-start = ((), (), s32[]{:S(2)}) async-start(), calls=%async_computation.2 | async-start | bytes 524288 | tf_op jit(solution)/shard_map/psum | solution.py:30
  124.8 155.2 %copy-start.1 = (f32[512,256]{1,0:T(8,128)S(1)}, f32[512,256]{1,0:T(8,128)}, u32[]{:S(2)}) copy-start(f32[512,256]{1,0:T(8,128)} %reduce-scatter.2.cloned.1.call-done) | copy-start | bytes 1572868
  127.8 167.4 %all-gather.2.cloned.1.call-start = ((), (), s32[]{:S(2)}) async-start(), calls=%async_computation.3 | async-start | bytes 8912896 | tf_op jit(solution)/shard_map/all_gather | solution.py:26
Sparse Core Ops, SparseCore 0:
  18.6 106.1 reduce-scatter.1
  128.8 89.3 all-reduce.2
  220.4 74.7 all-gather.1
where the time goes:
time: 320 us; the launch traced here: 319 us
  waiting for transfers between devices  209 us (65%)
  other arithmetic  55.4 us (17%)
  matrix products  32.2 us (10%)
  between operations  15.2 us (5%)
  local copies, waits for them, and re-layouts  6.96 us (2%)
    reduce_scatter x1, waiting for transfers between devices, local(): lax.psum_scatter(jnp.dot(sample_rows, test_matrix, precision=highest, pre...  106 us
    psum x1, waiting for transfers between devices, local(): gram_one = lax.psum(local_gram(sketch), 'tm')  89.7 us
    another operation x6, other arithmetic, local(): factor_one = jnp.linalg.cholesky(gram_one)  34 us
    another operation x3, other arithmetic, local(): jax.scipy.linalg.solve_triangular(factor_one, sketch.T, lower=True)  19.7 us
    dot_general x1, matrix products, local(): jnp.einsum('rk,rs->ks', lax.all_gather(sketch, 'tm', axis=0, tiled=True),...  16.2 us
    all_gather x1, waiting for transfers between devices, local(): lax.all_gather(sketch, 'tm', axis=0, tiled=True)  12.7 us
    dot_general x1, matrix products, local(): jnp.dot(sample_rows, test_matrix, precision=highest, preferred_element_ty...  10.4 us
  transfers between devices with their start and end apart: 3, of which 3 were waited for; matrix products, arithmetic and copies ran while one was open for 20% of the time, Pallas kernels for 0%

commit v1 on v0

v1 whole, which is shorter than its diff:
```python
import math

import jax
import jax.numpy as jnp
from jax import lax
from jax.experimental import pallas as pl
from jax.experimental.pallas import tpu as pltpu
from jax.sharding import PartitionSpec as P

HIGHEST = lax.Precision.HIGHEST
VMEM = pl.BlockSpec(memory_space=pltpu.VMEM)
SMEM = pl.BlockSpec(memory_space=pltpu.SMEM)
SIDE = 64


def contract(a, b, dims):
    return lax.dot_general(
        a, b, (dims, ((), ())), precision=HIGHEST, preferred_element_type=jnp.float32
    )


def dot(a, b):
    return contract(a, b, ((1,), (0,)))


def split(v):
    high = v.astype(jnp.bfloat16)
    return high, (v - high.astype(jnp.float32)).astype(jnp.bfloat16)


def split_dot(a, b, dims=((1,), (0,))):
    (ah, al), (bh, bl) = split(a), split(b)

    def one(x, y):
        return lax.dot_general(x, y, (dims, ((), ())), preferred_element_type=jnp.float32)

    return one(ah, bh) + (one(ah, bl) + one(al, bh))


def factor_block(x, off):
    count = len(x)
    sub = lax.broadcasted_iota(jnp.int32, (8, 128), 0)

    def spread(v):
        return jnp.broadcast_to(v, (8, 128))

    for p in range(count):
        base = off + 8 * p
        cols = [[spread(x[t][:, base + j : base + j + 1]) for j in range(8)] for t in range(p, count)]
        d = [[spread(cols[0][j][i : i + 1, :]) for j in range(i + 1)] for i in range(8)]
        scale = []
        for j in range(8):
            scale.append(lax.rsqrt(d[j][j]))
            for i in range(j + 1, 8):
                d[i][j] = d[i][j] * scale[j]
            for i in range(j + 1, 8):
                for k in range(j + 1, i + 1):
                    d[i][k] = d[i][k] - d[i][j] * d[k][j]
        rows = []
        for j in range(8):
            r = spread(x[p][j : j + 1, :])
            for k in range(j):
                r = r - d[j][k] * rows[k]
            rows.append(r * scale[j])
        out = rows[0]
        for j in range(1, 8):
            out = jnp.where(sub == j, rows[j], out)
        x[p] = out
        for t in range(p + 1, count):
            done = []
            acc = x[t]
            for j in range(8):
                v = cols[t - p][j]
                for k in range(j):
                    v = v - d[j][k] * done[k]
                v = v * scale[j]
                done.append(v)
                acc = acc - v * rows[j]
            x[t] = acc
    return x


def eliminate(work, inv, j):
    rank = work.shape[0]
    lane = lax.broadcasted_iota(jnp.int32, (8, 128), 1)
    sub = lax.broadcasted_iota(jnp.int32, (8, 128), 0)
    start, stop = j * SIDE, (j + 1) * SIDE
    off = start % 128
    other = SIDE - off
    lanes = start // 128 * 128
    inside = (lane >= off) & (lane < off + SIDE)
    tiles = []
    for t in range(SIDE // 8):
        v = work[start + 8 * t : start + 8 * t + 8, lanes : lanes + 128]
        tiles.append(jnp.where(inside, v, jnp.where(lane - other == sub + 8 * t, 1.0, 0.0)))
    tile = jnp.concatenate(factor_block(tiles, off), 0)
    lane_of = lax.broadcasted_iota(jnp.int32, (SIDE, 128), 1)
    tile = jnp.where((lane_of >= other) & (lane_of < other + SIDE), tile, 0.0)
    rows = jnp.concatenate([work[start:stop, :], inv[start:stop, :]], 1)
    zero = jnp.zeros_like(rows)
    rows = jnp.concatenate([rows, zero] if other == 0 else [zero, rows], 0)
    panel = dot(tile, rows)
    inv[start:stop, :] = panel[:, rank:]
    if stop < rank:
        low = stop // 128 * 128
        left = panel[:, low:rank]
        column = lax.broadcasted_iota(jnp.int32, left.shape, 1) + low
        left = jnp.where(column >= stop, left, 0.0)
        update = contract(left, panel, ((0,), (0,)))
        work[low:, :] = work[low:, :] - update[:, :rank]
        inv[low:, :] = inv[low:, :] - update[:, rank:]


def call(kernel, out_shapes, args, scratch=(), flops=0, grant=12, alias=None):
    shapes = [jax.ShapeDtypeStruct(s, jnp.float32) for s in out_shapes]
    moved = 4 * sum(math.prod(a.shape) for a in (*args, *shapes))
    return pl.pallas_call(
        kernel,
        out_shape=shapes,
        in_specs=[SMEM if a.dtype == jnp.int32 else VMEM for a in args],
        out_specs=[VMEM] * len(shapes),
        scratch_shapes=[pltpu.VMEM(s, jnp.float32) for s in scratch],
        cost_estimate=pl.CostEstimate(flops=flops, bytes_accessed=moved, transcendentals=0),
        input_output_aliases=alias or {},
        compiler_params=pltpu.CompilerParams(vmem_limit_bytes=grant << 20),
    )(*args)


def blocks_of(samples, which, block, me):
    count = len(which)

    def kernel(me_ref, source, *refs):
        outs, done = refs[:count], refs[count]
        copies = []
        for k, (bits, out) in enumerate(zip(which, outs)):
            at = pl.multiple_of((me_ref[0] ^ bits) * block, block)
            copies.append(pltpu.make_async_copy(source.at[pl.ds(at, block), :], out, done.at[k]))
        for c in copies:
            c.start()
        for c in copies:
            c.wait()

    shape = jax.ShapeDtypeStruct((block, samples.shape[1]), jnp.float32)
    return pl.pallas_call(
        kernel,
        out_shape=[shape] * count,
        in_specs=[SMEM, pl.BlockSpec(memory_space=pltpu.HBM)],
        out_specs=[VMEM] * count,
        scratch_shapes=[pltpu.SemaphoreType.DMA((count,))],
        cost_estimate=pl.CostEstimate(
            flops=0, bytes_accessed=8 * count * math.prod(shape.shape), transcendentals=0
        ),
        compiler_params=pltpu.CompilerParams(vmem_limit_bytes=12 << 20),
        name="blocks",
    )(me, samples)


def sketch_of(parts, mixers, half, extra, last=False):
    count, blend = len(parts), len(mixers)
    rows, rank = parts[0].shape[0] // 2, mixers[0].shape[1]

    def kernel(*refs):
        ins = refs[: count + blend + len(extra)]
        at = slice(half * rows, (half + 1) * rows)
        left = jnp.concatenate([r[at, :] for r in ins[:count]], 1)
        mixer = jnp.concatenate([r[...] for r in ins[count : count + blend]], 0)
        total = split_dot(left, mixer)
        for r in ins[count + blend :]:
            total = total + r[...]
        refs[len(ins)][...] = total
        if last:
            refs[-1][...] = total.T

    shapes = [(rows, rank), (rank, rows)] if last else [(rows, rank)]
    depth = count * parts[0].shape[1]
    return call(kernel, shapes, [*parts, *mixers, *extra], flops=6 * rows * rank * depth)


def gram_halves(rows, turned, me):
    rank = turned[0].shape[0]
    half = rank // 2
    count = len(rows)

    def kernel(me_ref, *refs):
        keep, send, work = refs[2 * count :]
        left = jnp.concatenate([r[...] for r in refs[count : 2 * count]], 1)
        work[...] = dot(left, jnp.concatenate([r[...] for r in refs[:count]], 0))
        low = me_ref[0] & 1
        keep[...] = work[pl.ds(pl.multiple_of(low * half, half), half), :]
        send[...] = work[pl.ds(pl.multiple_of((1 - low) * half, half), half), :]

    return call(
        kernel, [(half, rank)] * 2, [me, *rows, *turned], [(rank, rank)],
        flops=12 * rank * rank * count * rows[0].shape[0],
    )


def add_halves(a, b, me):
    half, rank = a.shape[0] // 2, a.shape[1]

    def kernel(me_ref, a_ref, b_ref, keep, send):
        mid = (me_ref[0] >> 1) & 1
        for out, which in ((keep, mid), (send, 1 - mid)):
            at = pl.ds(pl.multiple_of(which * half, half), half)
            out[...] = a_ref[at, :] + b_ref[at, :]

    return call(kernel, [(half, rank)] * 2, [me, a, b])


def add_all(arrays):
    def kernel(*refs):
        total = refs[0][...]
        for r in refs[1:-1]:
            total = total + r[...]
        refs[-1][...] = total

    return call(kernel, [arrays[0].shape], arrays)[0]


def inverse_factor(quarters, me):
    part, rank = quarters[0].shape
    square = [(rank, rank)] * 2

    def first(me_ref, *refs):
        work, inv = refs[4:]
        mid, low = (me_ref[0] >> 1) & 1, me_ref[0] & 1
        for d in range(4):
            at = ((low ^ (d & 1)) * 2 + (mid ^ (d >> 1))) * part
            work[pl.ds(pl.multiple_of(at, part), part), :] = refs[d][...]
        wide = lax.broadcasted_iota(jnp.int32, (rank, rank), 1)
        tall = lax.broadcasted_iota(jnp.int32, (rank, rank), 0)
        inv[...] = jnp.where(wide == tall, 1.0, 0.0)
        eliminate(work, inv, 0)

    def later(j):
        def kernel(work_in, inv_in, work, inv):
            eliminate(work, inv, j)

        return kernel

    state = call(first, square, [me, *quarters], flops=10**9)
    for j in range(1, rank // SIDE):
        state = call(later(j), square, state, flops=10**9, alias={0: 0, 1: 1})
    return state[1]


def basis_of(sketch_rows, inverse, root):
    count, (rows, rank) = len(sketch_rows), sketch_rows[0].shape

    def kernel(*refs):
        left = jnp.concatenate([r[...] for r in refs[:count]], 0)
        refs[-1][...] = split_dot(left, refs[count][...], ((1,), (1,))) * root

    return call(
        kernel, [(count * rows, rank)], [*sketch_rows, inverse],
        flops=6 * count * rows * rank * rank,
    )[0]


def project(turned, parts, half, previous, last=False):
    count, rank = len(parts), turned.shape[0]
    cols = parts[0].shape[1]

    depth = turned.shape[1]

    def kernel(*refs):
        at = slice(half * depth, (half + 1) * depth)
        right = jnp.concatenate([r[at, :] for r in refs[1 : 1 + count]], 1)
        total = split_dot(refs[0][...], right)
        if previous is not None:
            total = total + refs[1 + count][...]
        if not last:
            refs[-1][...] = total
            return
        piece = [total[:, d * cols : (d + 1) * cols] for d in range(count)]
        refs[-3][...] = piece[0]
        refs[-2][...] = piece[2]
        refs[-1][:, :cols] = piece[1]
        refs[-1][:, cols:] = piece[3]

    shapes = [(rank, cols), (rank, cols), (rank, 2 * cols)] if last else [(rank, count * cols)]
    extra = [] if previous is None else [previous]
    return call(
        kernel, shapes, [turned, *parts, *extra],
        flops=6 * rank * count * cols * turned.shape[1],
    )


def pair_sum(second, sent):
    cols = second.shape[1]

    def kernel(a, b, out):
        out[...] = a[...] + b[:, cols:]

    return call(kernel, [second.shape], [second, sent])[0]


def coordinates_of(inverse, first, sent, across):
    cols = first.shape[1]

    def kernel(inv, a, b, c, out):
        out[...] = split_dot(inv[...], a[...] + b[:, :cols] + c[...])

    rank = inverse.shape[0]
    return call(
        kernel, [first.shape], [inverse, first, sent, across],
        flops=6 * rank * rank * cols,
    )[0]


def make_local(size):
    quads = size // 4

    def swap(x, bit):
        return lax.ppermute(x, "tm", [(i, i ^ bit) for i in range(size)])

    def total_gram(keep, sent, me):
        keep, send = add_halves(keep, sent, me)
        part = add_all([keep, swap(send, 2)])
        if quads <= 4:
            part = add_all([part] + [swap(part, 4 * e) for e in range(1, quads)])
        else:
            bit = 4
            while bit < size:
                part = add_all([part, swap(part, bit)])
                bit *= 2
        other = swap(part, 2)
        return [part, swap(part, 1), other, swap(other, 1)]

    def local(samples, test_matrix):
        return inner(samples, test_matrix)

    def inner(samples, test_matrix):
        place = lax.axis_index("tm")
        me = place.astype(jnp.int32).reshape(1)
        channels, _ = samples.shape
        block = channels // size

        order = list(reversed(range(quads)))
        mail = {}
        sends = [[(order[0], d) for d in (2, 3, 1)], [(e, d) for e in order[1:] for d in (2, 3, 1)]]
        for wanted in sends:
            found = blocks_of(samples, [4 * e + d for e, d in wanted], block, me)
            for (e, d), x in zip(wanted, found):
                mail[e, d] = swap(x, d)
        stay = blocks_of(samples, [4 * e for e in range(quads)], block, me)

        other = swap(test_matrix, 2)
        across = swap(test_matrix, 1)
        diagonal = swap(other, 1)
        mixers = [test_matrix, across, other, diagonal]

        parts = [None] * quads
        inbox = {(e, h): [] for e in range(quads) for h in (0, 1)}
        mine, turned = [None, None], [None, None]
        for e in order:
            parts[e] = [stay[e]] + [mail[e, d] for d in (1, 2, 3)]
            for h in (0, 1):
                found = sketch_of(parts[e], mixers, h, inbox[e, h], last=e == 0)
                if e:
                    step = e & -e
                    inbox[e - step, h].append(swap(found[0], 4 * step))
                else:
                    mine[h], turned[h] = found

        keep, send = gram_halves(mine, turned, me)
        quarters = total_gram(keep, swap(send, 1), me)
        inverse = inverse_factor(quarters, me)
        basis = basis_of(mine, inverse, float(channels) ** 0.5)

        held = {(0, h): turned[h] for h in (0, 1)}
        bit = quads // 2
        while bit >= 1:
            for e, h in sorted(held):
                held[e + bit, h] = swap(held[e, h], 4 * bit)
            bit //= 2
        projected = None
        sequence = sorted(held, key=lambda k: (k[1], bin(k[0]).count("1"), -k[0]))
        for e, h in sequence:
            last = (e, h) == sequence[-1]
            projected = project(held[e, h], parts[e], h, projected, last)
            if not last:
                projected = projected[0]
        first, second, send = projected
        sent = swap(send, 1)
        second = pair_sum(second, sent)
        fold = swap(second, 2)
        return basis, coordinates_of(inverse, first, sent, fold)

    return local


def solution(mesh):
    placed = (P("groups", "tm"), P(("groups", "tm"), None))
    return jax.shard_map(
        make_local(mesh.shape["tm"]),
        mesh=mesh,
        in_specs=placed,
        out_specs=(P(("groups", "tm"), None), P("groups", "tm")),
        check_vma=False,
    )
```

time: 320 us -> 138 us (0.43)
  waiting for transfers between devices: 209 us -> 76.6 us
  other arithmetic: 55.4 us -> 0 us
  starting transfers between devices: 0.3 us -> 38.6 us
  matrix products: 32.2 us -> 0 us
  Pallas kernels: 0 us -> 19.3 us
  between operations: 15.2 us -> 0.95 us
  local copies, waits for them, and re-layouts: 6.96 us -> 2.19 us
    reduce_scatter x1 -> x0, waiting for transfers between devices: 106 us -> none  [local(): lax.psum_scatter(jnp.dot(sample_rows, test_matrix, precision=highest, pre...]
    psum x1 -> x0, waiting for transfers between devices: 89.7 us -> none  [local(): gram_one = lax.psum(local_gram(sketch), 'tm')]
    ppermute x0 -> x37, waiting for transfers between devices: none -> 76.6 us  [swap(): return lax.ppermute(x, 'tm', [(i, i ^ bit) for i in range(size)])]
    another operation x10 -> x0, other arithmetic: 54.4 us -> none  [the longest x6 34 us: local(): factor_one = jnp.linalg.cholesky(gram_one)]
    ppermute x0 -> x37, starting transfers between devices: none -> 38.6 us  [swap(): return lax.ppermute(x, 'tm', [(i, i ^ bit) for i in range(size)])]
    dot_general x3 -> x0, matrix products: 29.6 us -> none  [the longest x1 16.2 us: local(): jnp.einsum('rk,rs->ks', lax.all_gather(sketch, 'tm', axis=0, tiled=True),...]
    pallas_call x0 -> x30, Pallas kernels: none -> 19.3 us  [the longest x27 18.8 us: call(): pl.pallas_call(kernel, out_shape=shapes, in_specs=[SMEM if a.dtype == jnp...]
    all_gather x1 -> x0, waiting for transfers between devices: 12.7 us -> none  [local(): lax.all_gather(sketch, 'tm', axis=0, tiled=True)]
  transfers between devices with their start and end apart: 3 -> 37, of which waited for: 3 -> 21; matrix products, arithmetic and copies ran while one was open for 20% -> 0% of each run, Pallas kernels for 0% -> 13%
where the time goes in v1:
time: 138 us
  waiting for transfers between devices  76.6 us (56%)
  starting transfers between devices  38.6 us (28%)
  Pallas kernels  19.3 us (14%)
  local copies, waits for them, and re-layouts  2.19 us (2%)
    ppermute x37, waiting for transfers between devices, swap(): return lax.ppermute(x, 'tm', [(i, i ^ bit) for i in range(size)])  76.6 us
    ppermute x37, starting transfers between devices, swap(): return lax.ppermute(x, 'tm', [(i, i ^ bit) for i in range(size)])  38.6 us
    pallas_call x27, Pallas kernels, call(): pl.pallas_call(kernel, out_shape=shapes, in_specs=[SMEM if a.dtype == jnp...  18.8 us
  transfers between devices with their start and end apart: 37, of which 21 were waited for; matrix products, arithmetic and copies ran while one was open for 0% of the time, Pallas kernels for 13%

profile of v1, /device:TPU:0, one launch (start us, length us, event | category | flops | bytes accessed | tf_op | source)
XLA Modules:
  0.0 137.6 jit_solution(8430960668070858807)
XLA Ops:
  0.6 3.1 %collective-permute-start.4 = (f32[128,256]{1,0:T(8,128)}, f32[128,256]{1,0:T(8,128)S(1)}, u32[]{:S(2)}, u32[]{:S(2)}) collective-permute-start(f32[128,256]{1,0:T(8,128)} %refs_4_.15), channel_id=1, source_target_pairs={{0,2},{1,3},{2,0},{3,1},{4,6},{5,7},{6,4},{7,5},{8,10},{9,11},{10,... | collective-permute-start | bytes 393224 | tf_op jit(solution)/shard_map/ppermute | solution.py:315
  3.7 2.2 %copy-done = f32[8192,128]{1,0:T(8,128)S(1)} copy-done((f32[8192,128]{1,0:T(8,128)S(1)}, f32[8192,128]{1,0:T(8,128)}, u32[]{:S(2)}) %copy-start) | copy-done | bytes 4194328
  6.1 0.9 collective-permute-start.11
  6.9 1.2 collective-permute-start.9
  8.2 0.5 collective-permute-start.5
  9.0 0.6 collective-permute-done.3.refs_5_
  9.9 1.2 collective-permute-start.7
  11.1 4.1 %collective-permute-done.10.refs_2_.refs_3_ = f32[512,128]{1,0:T(8,128)S(1)} collective-permute-done((f32[512,128]{1,0:T(8,128)S(1)}, f32[512,128]{1,0:T(8,128)S(1)}, u32[]{:S(2)}, u32[]{:S(2)}) %collective-permute-start.10) | collective-permute-done | bytes 262176 | tf_op jit(solution)/shard_map/ppermute | solution.py:315
  15.2 3.3 %collective-permute-done.11.refs_3_.refs_4_ = f32[512,128]{1,0:T(8,128)S(1)} collective-permute-done((f32[512,128]{1,0:T(8,128)S(1)}, f32[512,128]{1,0:T(8,128)S(1)}, u32[]{:S(2)}, u32[]{:S(2)}) %collective-permute-start.11) | collective-permute-done | bytes 262176 | tf_op jit(solution)/shard_map/ppermute | solution.py:315
  18.5 1.8 %collective-permute-start.15 = (f32[512,128]{1,0:T(8,128)S(1)}, f32[512,128]{1,0:T(8,128)S(1)}, u32[]{:S(2)}, u32[]{:S(2)}) collective-permute-start(f32[512,128]{1,0:T(8,128)S(1)} %get-tuple-element.50), channel_id=1, source_target_pairs={{0,2},{1,3},{2,0},{3,1},{4,6},{5,7},{6,4},{7,5},{8,10},{9,11},{10,... | collective-permute-start | bytes 786440 | tf_op jit(solution)/shard_map/ppermute | solution.py:315
  20.4 1.6 %collective-permute-start.16 = (f32[512,128]{1,0:T(8,128)S(1)}, f32[512,128]{1,0:T(8,128)S(1)}, u32[]{:S(2)}, u32[]{:S(2)}) collective-permute-start(f32[512,128]{1,0:T(8,128)S(1)} %get-tuple-element.51), channel_id=1, source_target_pairs={{0,3},{1,2},{2,1},{3,0},{4,7},{5,6},{6,5},{7,4},{8,11},{9,10},{10,... | collective-permute-start | bytes 786440 | tf_op jit(solution)/shard_map/ppermute | solution.py:315
  22.3 0.4 shard_map.41
  22.7 3.7 %collective-permute-done.7.refs_2_.refs_3_ = f32[512,128]{1,0:T(8,128)S(1)} collective-permute-done((f32[512,128]{1,0:T(8,128)S(1)}, f32[512,128]{1,0:T(8,128)S(1)}, u32[]{:S(2)}, u32[]{:S(2)}) %collective-permute-start.7) | collective-permute-done | bytes 262176 | tf_op jit(solution)/shard_map/ppermute | solution.py:315
  26.5 1.6 %collective-permute-start.12 = (f32[256,256]{1,0:T(8,128)S(1)}, f32[256,256]{1,0:T(8,128)S(1)}, u32[]{:S(2)}, u32[]{:S(2)}) collective-permute-start(f32[256,256]{1,0:T(8,128)S(1)} %shard_map.41), channel_id=1, source_target_pairs={{0,4},{1,5},{2,6},{3,7},{4,0},{5,1},{6,2},{7,3},{8,12},{9,13},{10,... | collective-permute-start | bytes 786440 | tf_op jit(solution)/shard_map/ppermute | solution.py:315
  28.0 0.4 shard_map.45
  28.4 0.5 collective-permute-start.18
  29.0 3.1 %collective-permute-done.15.refs_2_.refs_3_ = f32[512,128]{1,0:T(8,128)S(1)} collective-permute-done((f32[512,128]{1,0:T(8,128)S(1)}, f32[512,128]{1,0:T(8,128)S(1)}, u32[]{:S(2)}, u32[]{:S(2)}) %collective-permute-start.15) | collective-permute-done | bytes 262176 | tf_op jit(solution)/shard_map/ppermute | solution.py:315
  32.1 3.3 %collective-permute-done.16.refs_3_.refs_4_ = f32[512,128]{1,0:T(8,128)S(1)} collective-permute-done((f32[512,128]{1,0:T(8,128)S(1)}, f32[512,128]{1,0:T(8,128)S(1)}, u32[]{:S(2)}, u32[]{:S(2)}) %collective-permute-start.16) | collective-permute-done | bytes 262176 | tf_op jit(solution)/shard_map/ppermute | solution.py:315
  35.4 1.8 %collective-permute-start.1 = (f32[512,128]{1,0:T(8,128)S(1)}, f32[512,128]{1,0:T(8,128)S(1)}, u32[]{:S(2)}, u32[]{:S(2)}) collective-permute-start(f32[512,128]{1,0:T(8,128)S(1)} %get-tuple-element.38), channel_id=1, source_target_pairs={{0,2},{1,3},{2,0},{3,1},{4,6},{5,7},{6,4},{7,5},{8,10},{9,11},{10,... | collective-permute-start | bytes 786440 | tf_op jit(solution)/shard_map/ppermute | solution.py:315
  37.2 0.4 shard_map.43
  37.6 3.4 %collective-permute-done.8.refs_3_.refs_4_ = f32[512,128]{1,0:T(8,128)S(1)} collective-permute-done((f32[512,128]{1,0:T(8,128)S(1)}, f32[512,128]{1,0:T(8,128)S(1)}, u32[]{:S(2)}, u32[]{:S(2)}) %collective-permute-start.8) | collective-permute-done | bytes 262176 | tf_op jit(solution)/shard_map/ppermute | solution.py:315
  41.0 1.9 %collective-permute-start.2 = (f32[512,128]{1,0:T(8,128)S(1)}, f32[512,128]{1,0:T(8,128)S(1)}, u32[]{:S(2)}, u32[]{:S(2)}) collective-permute-start(f32[512,128]{1,0:T(8,128)S(1)} %get-tuple-element.39), channel_id=1, source_target_pairs={{0,3},{1,2},{2,1},{3,0},{4,7},{5,6},{6,5},{7,4},{8,11},{9,10},{10,... | collective-permute-start | bytes 786440 | tf_op jit(solution)/shard_map/ppermute | solution.py:315
  42.9 1.9 %collective-permute-start.17 = (f32[256,256]{1,0:T(8,128)S(1)}, f32[256,256]{1,0:T(8,128)S(1)}, u32[]{:S(2)}, u32[]{:S(2)}) collective-permute-start(f32[256,256]{1,0:T(8,128)S(1)} %shard_map.43), channel_id=1, source_target_pairs={{0,4},{1,5},{2,6},{3,7},{4,0},{5,1},{6,2},{7,3},{8,12},{9,13},{10,... | collective-permute-start | bytes 786440 | tf_op jit(solution)/shard_map/ppermute | solution.py:315
  44.8 0.4 shard_map.42
  45.2 2.7 %collective-permute-start.13 = (f32[256,256]{1,0:T(8,128)S(1)}, f32[256,256]{1,0:T(8,128)S(1)}, u32[]{:S(2)}, u32[]{:S(2)}) collective-permute-start(f32[256,256]{1,0:T(8,128)S(1)} %shard_map.42), channel_id=1, source_target_pairs={{0,8},{1,9},{2,10},{3,11},{4,12},{5,13},{6,14},{7,15},{8,0},{9,1},... | collective-permute-start | bytes 786440 | tf_op jit(solution)/shard_map/ppermute | solution.py:315
  47.9 0.4 shard_map.47
  48.3 0.4 shard_map.46
  48.7 0.5 collective-permute-start.20
  49.2 2.3 %collective-permute-start.19 = (f32[256,256]{1,0:T(8,128)S(1)}, f32[256,256]{1,0:T(8,128)S(1)}, u32[]{:S(2)}, u32[]{:S(2)}) collective-permute-start(f32[256,256]{1,0:T(8,128)S(1)} %shard_map.46), channel_id=1, source_target_pairs={{0,8},{1,9},{2,10},{3,11},{4,12},{5,13},{6,14},{7,15},{8,0},{9,1},... | collective-permute-start | bytes 786440 | tf_op jit(solution)/shard_map/ppermute | solution.py:315
  51.7 5.4 %collective-permute-done.17.refs_9_ = f32[256,256]{1,0:T(8,128)S(1)} collective-permute-done((f32[256,256]{1,0:T(8,128)S(1)}, f32[256,256]{1,0:T(8,128)S(1)}, u32[]{:S(2)}, u32[]{:S(2)}) %collective-permute-start.17) | collective-permute-done | bytes 262176 | tf_op jit(solution)/shard_map/ppermute | solution.py:315
  57.1 4.0 %collective-permute-done.13.refs_8_ = f32[256,256]{1,0:T(8,128)S(1)} collective-permute-done((f32[256,256]{1,0:T(8,128)S(1)}, f32[256,256]{1,0:T(8,128)S(1)}, u32[]{:S(2)}, u32[]{:S(2)}) %collective-permute-start.13) | collective-permute-done | bytes 262176 | tf_op jit(solution)/shard_map/ppermute | solution.py:315
  61.1 0.5 shard_map.44
  61.6 6.0 %collective-permute-done.20.refs_9_ = f32[256,256]{1,0:T(8,128)S(1)} collective-permute-done((f32[256,256]{1,0:T(8,128)S(1)}, f32[256,256]{1,0:T(8,128)S(1)}, u32[]{:S(2)}, u32[]{:S(2)}) %collective-permute-start.20) | collective-permute-done | bytes 262176 | tf_op jit(solution)/shard_map/ppermute | solution.py:315
  67.6 10.3 %collective-permute-done.19.refs_8_ = f32[256,256]{1,0:T(8,128)S(1)} collective-permute-done((f32[256,256]{1,0:T(8,128)S(1)}, f32[256,256]{1,0:T(8,128)S(1)}, u32[]{:S(2)}, u32[]{:S(2)}) %collective-permute-start.19) | collective-permute-done | bytes 262176 | tf_op jit(solution)/shard_map/ppermute | solution.py:315
  77.9 0.5 shard_map.48
  78.4 0.7 shard_map.49
  79.2 1.3 collective-permute-done.21.b_ref
  80.6 4.4 %collective-permute-start.22 = (f32[64,256]{1,0:T(8,128)S(1)}, f32[64,256]{1,0:T(8,128)S(1)}, u32[]{:S(2)}, u32[]{:S(2)}) collective-permute-start(f32[64,256]{1,0:T(8,128)S(1)} %get-tuple-element.59), channel_id=1, source_target_pairs={{0,2},{1,3},{2,0},{3,1},{4,6},{5,7},{6,4},{7,5},{8,10},{9,11},{10,... | collective-permute-start | bytes 196616 | tf_op jit(solution)/shard_map/ppermute | solution.py:315
  85.0 2.7 %collective-permute-start.34 = (f32[256,256]{1,0:T(8,128)S(1)}, f32[256,256]{1,0:T(8,128)S(1)}, u32[]{:S(2)}, u32[]{:S(2)}) collective-permute-start(f32[256,256]{1,0:T(8,128)S(1)} %get-tuple-element.54.refs_2_.refs_0_), channel_id=1, source_target_pairs={{0,4},{1,5},{2,6},{3,7},{4,0},{5,1},{6,2},{7,3},{8,12},{9,13},{10,... | collective-permute-start | bytes 786440 | tf_op jit(solution)/shard_map/ppermute | solution.py:315
  87.7 1.5 %collective-permute-done.32.refs_0_ = f32[256,256]{1,0:T(8,128)S(1)} collective-permute-done((f32[256,256]{1,0:T(8,128)S(1)}, f32[256,256]{1,0:T(8,128)S(1)}, u32[]{:S(2)}, u32[]{:S(2)}) %collective-permute-start.32) | collective-permute-done | bytes 262176 | tf_op jit(solution)/shard_map/ppermute | solution.py:315
  89.2 2.1 %collective-permute-start.23 = (f32[64,256]{1,0:T(8,128)S(1)}, f32[64,256]{1,0:T(8,128)S(1)}, u32[]{:S(2)}, u32[]{:S(2)}) collective-permute-start(f32[64,256]{1,0:T(8,128)S(1)} %shard_map.51.refs_0_), channel_id=1, source_target_pairs={{0,4},{1,5},{2,6},{3,7},{4,0},{5,1},{6,2},{7,3},{8,12},{9,13},{10,... | collective-permute-start | bytes 196616 | tf_op jit(solution)/shard_map/ppermute | solution.py:315
  91.4 2.1 %collective-permute-done.29.refs_0_ = f32[256,256]{1,0:T(8,128)S(1)} collective-permute-done((f32[256,256]{1,0:T(8,128)S(1)}, f32[256,256]{1,0:T(8,128)S(1)}, u32[]{:S(2)}, u32[]{:S(2)}) %collective-permute-start.29) | collective-permute-done | bytes 262176 | tf_op jit(solution)/shard_map/ppermute | solution.py:315
  93.5 12.6 %collective-permute-done.23.refs_1_ = f32[64,256]{1,0:T(8,128)S(1)} collective-permute-done((f32[64,256]{1,0:T(8,128)S(1)}, f32[64,256]{1,0:T(8,128)S(1)}, u32[]{:S(2)}, u32[]{:S(2)}) %collective-permute-start.23) | collective-permute-done | bytes 65568 | tf_op jit(solution)/shard_map/ppermute | solution.py:315
  106.1 0.6 collective-permute-start.24
  106.7 6.2 %collective-permute-done.24.refs_2_ = f32[64,256]{1,0:T(8,128)S(1)} collective-permute-done((f32[64,256]{1,0:T(8,128)S(1)}, f32[64,256]{1,0:T(8,128)S(1)}, u32[]{:S(2)}, u32[]{:S(2)}) %collective-permute-start.24) | collective-permute-done | bytes 65568 | tf_op jit(solution)/shard_map/ppermute | solution.py:315
  112.9 1.7 %collective-permute-start.25 = (f32[64,256]{1,0:T(8,128)S(1)}, f32[64,256]{1,0:T(8,128)S(1)}, u32[]{:S(2)}, u32[]{:S(2)}) collective-permute-start(f32[64,256]{1,0:T(8,128)S(1)} %shard_map.51.refs_0_), channel_id=1, source_target_pairs={{0,12},{1,13},{2,14},{3,15},{4,8},{5,9},{6,10},{7,11},{8,4},{9,5},... | collective-permute-start | bytes 196616 | tf_op jit(solution)/shard_map/ppermute | solution.py:315
  115.0 4.1 %collective-permute-done.25.refs_3_ = f32[64,256]{1,0:T(8,128)S(1)} collective-permute-done((f32[64,256]{1,0:T(8,128)S(1)}, f32[64,256]{1,0:T(8,128)S(1)}, u32[]{:S(2)}, u32[]{:S(2)}) %collective-permute-start.25) | collective-permute-done | bytes 65568 | tf_op jit(solution)/shard_map/ppermute | solution.py:315
  119.1 0.9 collective-permute-start.27
  120.0 0.4 shard_map.59.refs_5_
  120.4 0.4 shard_map.60.refs_5_
  120.8 0.4 shard_map.61.refs_5_
  121.2 0.4 shard_map.62.refs_5_
  121.6 0.4 shard_map.63.refs_5_
  122.0 0.4 shard_map.64.refs_5_
  122.4 0.4 shard_map.65
  122.9 0.5 collective-permute-start.26
  123.5 1.0 collective-permute-done.26.refs_1_
  124.7 2.7 %shard_map.53 = (f32[256,256]{1,0:T(8,128)S(1)}, f32[256,256]{1,0:T(8,128)S(1)}) custom-call(s32[1]{0:T(128)} %bitcast.me_ref, f32[64,256]{1,0:T(8,128)S(1)} %shard_map.52.refs_0_, f32[64,256]{1,0:T(8,128)S(1)} %collective-permute-done.26.refs_1_, f32[64,256]{1,0:T(8,128)S(1)} %collective-permute-done.27.refs_2_, f32[64,256]{1,0:T(8,128)S(1)} %collective-permute-done.28.refs_3_), custom_call_target="tpu_custom_call" | custom-call | flops 1000000000 | bytes 786436 | tf_op jit(solution)/shard_map/pallas_call | solution.py:117
  127.4 2.4 %shard_map.54 = (f32[256,256]{1,0:T(8,128)S(1)}, f32[256,256]{1,0:T(8,128)S(1)}) custom-call(f32[256,256]{1,0:T(8,128)S(1)} %get-tuple-element.60.work_in, f32[256,256]{1,0:T(8,128)S(1)} %get-tuple-element.61.inv_in), custom_call_target="tpu_custom_call", output_to_operand_aliasing={{0}: (0, {}), {1}: (1, {})} | custom-call | flops 1000000000 | bytes 1048576 | tf_op jit(solution)/shard_map/pallas_call | solution.py:117
  129.9 1.2 collective-permute-start.36
  131.1 2.4 %shard_map.55 = (f32[256,256]{1,0:T(8,128)S(1)}, f32[256,256]{1,0:T(8,128)S(1)}) custom-call(f32[256,256]{1,0:T(8,128)S(1)} %get-tuple-element.62.work_in, f32[256,256]{1,0:T(8,128)S(1)} %get-tuple-element.63.inv_in), custom_call_target="tpu_custom_call", output_to_operand_aliasing={{0}: (0, {}), {1}: (1, {})} | custom-call | flops 1000000000 | bytes 1048576 | tf_op jit(solution)/shard_map/pallas_call | solution.py:117
  133.5 2.0 %shard_map.56 = (f32[256,256]{1,0:T(8,128)S(1)}, f32[256,256]{1,0:T(8,128)S(1)}) custom-call(f32[256,256]{1,0:T(8,128)S(1)} %get-tuple-element.64.work_in, f32[256,256]{1,0:T(8,128)S(1)} %get-tuple-element.65.inv_in), custom_call_target="tpu_custom_call", output_to_operand_aliasing={{0}: (0, {}), {1}: (1, {})} | custom-call | flops 1000000000 | bytes 1048576 | tf_op jit(solution)/shard_map/pallas_call | solution.py:117
  135.5 1.2 shard_map.57
  136.7 0.9 shard_map.67
  (44 shorter events, 2.5 us)
Async XLA Ops:
  0.6 7.6 %collective-permute-start.4 = (f32[128,256]{1,0:T(8,128)}, f32[128,256]{1,0:T(8,128)S(1)}, u32[]{:S(2)}, u32[]{:S(2)}) collective-permute-start(f32[128,256]{1,0:T(8,128)} %refs_4_.15), channel_id=1, source_target_pairs={{0,2},{1,3},{2,0},{3,1},{4,6},{5,7},{6,4},{7,5},{8,10},{9,11},{10,... | collective-permute-start | bytes 393224 | tf_op jit(solution)/shard_map/ppermute | solution.py:315
  3.7 2.2 %copy-start = (f32[8192,128]{1,0:T(8,128)S(1)}, f32[8192,128]{1,0:T(8,128)}, u32[]{:S(2)}) copy-start(f32[8192,128]{1,0:T(8,128)} %source.5) | copy-start | bytes 12582916
  5.9 2.3 %copy-start.1 = (f32[128,256]{1,0:T(8,128)S(1)}, f32[128,256]{1,0:T(8,128)}, u32[]{:S(2)}) copy-start(f32[128,256]{1,0:T(8,128)} %refs_4_.15) | copy-start | bytes 393220
  6.0 9.2 %collective-permute-start.10 = (f32[512,128]{1,0:T(8,128)S(1)}, f32[512,128]{1,0:T(8,128)S(1)}, u32[]{:S(2)}, u32[]{:S(2)}) collective-permute-start(f32[512,128]{1,0:T(8,128)S(1)} %get-tuple-element.46), channel_id=1, source_target_pairs={{0,2},{1,3},{2,0},{3,1},{4,6},{5,7},{6,4},{7,5},{8,10},{9,11},{10,... | collective-permute-start | bytes 786440 | tf_op jit(solution)/shard_map/ppermute | solution.py:315
  6.1 12.5 %collective-permute-start.11 = (f32[512,128]{1,0:T(8,128)S(1)}, f32[512,128]{1,0:T(8,128)S(1)}, u32[]{:S(2)}, u32[]{:S(2)}) collective-permute-start(f32[512,128]{1,0:T(8,128)S(1)} %get-tuple-element.47), channel_id=1, source_target_pairs={{0,3},{1,2},{2,1},{3,0},{4,7},{5,6},{6,5},{7,4},{8,11},{9,10},{10,... | collective-permute-start | bytes 786440 | tf_op jit(solution)/shard_map/ppermute | solution.py:315
  6.9 13.4 %collective-permute-start.9 = (f32[512,128]{1,0:T(8,128)S(1)}, f32[512,128]{1,0:T(8,128)S(1)}, u32[]{:S(2)}, u32[]{:S(2)}) collective-permute-start(f32[512,128]{1,0:T(8,128)S(1)} %get-tuple-element.45), channel_id=1, source_target_pairs={{0,1},{1,0},{2,3},{3,2},{4,5},{5,4},{6,7},{7,6},{8,9},{9,8},{10,11... | collective-permute-start | bytes 786440 | tf_op jit(solution)/shard_map/ppermute | solution.py:315
  8.2 1.3 collective-permute-start.3
  8.2 1.7 %collective-permute-start.5 = (f32[128,256]{1,0:T(8,128)S(1)}, f32[128,256]{1,0:T(8,128)S(1)}, u32[]{:S(2)}, u32[]{:S(2)}) collective-permute-start(f32[128,256]{1,0:T(8,128)S(1)} %collective-permute-done.4.refs_6_), channel_id=1, source_target_pairs={{0,1},{1,0},{2,3},{3,2},{4,5},{5,4},{6,7},{7,6},{8,9},{9,8},{10,11... | collective-permute-start | bytes 393224 | tf_op jit(solution)/shard_map/ppermute | solution.py:315
  9.5 12.6 %collective-permute-start.6 = (f32[512,128]{1,0:T(8,128)S(1)}, f32[512,128]{1,0:T(8,128)S(1)}, u32[]{:S(2)}, u32[]{:S(2)}) collective-permute-start(f32[512,128]{1,0:T(8,128)S(1)} %get-tuple-element.41), channel_id=1, source_target_pairs={{0,1},{1,0},{2,3},{3,2},{4,5},{5,4},{6,7},{7,6},{8,9},{9,8},{10,11... | collective-permute-start | bytes 786440 | tf_op jit(solution)/shard_map/ppermute | solution.py:315
  9.9 16.5 %collective-permute-start.7 = (f32[512,128]{1,0:T(8,128)S(1)}, f32[512,128]{1,0:T(8,128)S(1)}, u32[]{:S(2)}, u32[]{:S(2)}) collective-permute-start(f32[512,128]{1,0:T(8,128)S(1)} %get-tuple-element.42), channel_id=1, source_target_pairs={{0,2},{1,3},{2,0},{3,1},{4,6},{5,7},{6,4},{7,5},{8,10},{9,11},{10,... | collective-permute-start | bytes 786440 | tf_op jit(solution)/shard_map/ppermute | solution.py:315
  15.2 13.2 %collective-permute-start.14 = (f32[512,128]{1,0:T(8,128)S(1)}, f32[512,128]{1,0:T(8,128)S(1)}, u32[]{:S(2)}, u32[]{:S(2)}) collective-permute-start(f32[512,128]{1,0:T(8,128)S(1)} %get-tuple-element.49), channel_id=1, source_target_pairs={{0,1},{1,0},{2,3},{3,2},{4,5},{5,4},{6,7},{7,6},{8,9},{9,8},{10,11... | collective-permute-start | bytes 786440 | tf_op jit(solution)/shard_map/ppermute | solution.py:315
  18.5 13.5 %collective-permute-start.15 = (f32[512,128]{1,0:T(8,128)S(1)}, f32[512,128]{1,0:T(8,128)S(1)}, u32[]{:S(2)}, u32[]{:S(2)}) collective-permute-start(f32[512,128]{1,0:T(8,128)S(1)} %get-tuple-element.50), channel_id=1, source_target_pairs={{0,2},{1,3},{2,0},{3,1},{4,6},{5,7},{6,4},{7,5},{8,10},{9,11},{10,... | collective-permute-start | bytes 786440 | tf_op jit(solution)/shard_map/ppermute | solution.py:315
  20.4 15.0 %collective-permute-start.16 = (f32[512,128]{1,0:T(8,128)S(1)}, f32[512,128]{1,0:T(8,128)S(1)}, u32[]{:S(2)}, u32[]{:S(2)}) collective-permute-start(f32[512,128]{1,0:T(8,128)S(1)} %get-tuple-element.51), channel_id=1, source_target_pairs={{0,3},{1,2},{2,1},{3,0},{4,7},{5,6},{6,5},{7,4},{8,11},{9,10},{10,... | collective-permute-start | bytes 786440 | tf_op jit(solution)/shard_map/ppermute | solution.py:315
  22.1 18.9 %collective-permute-start.8 = (f32[512,128]{1,0:T(8,128)S(1)}, f32[512,128]{1,0:T(8,128)S(1)}, u32[]{:S(2)}, u32[]{:S(2)}) collective-permute-start(f32[512,128]{1,0:T(8,128)S(1)} %get-tuple-element.43), channel_id=1, source_target_pairs={{0,3},{1,2},{2,1},{3,0},{4,7},{5,6},{6,5},{7,4},{8,11},{9,10},{10,... | collective-permute-start | bytes 786440 | tf_op jit(solution)/shard_map/ppermute | solution.py:315
  26.5 16.5 %collective-permute-start.12 = (f32[256,256]{1,0:T(8,128)S(1)}, f32[256,256]{1,0:T(8,128)S(1)}, u32[]{:S(2)}, u32[]{:S(2)}) collective-permute-start(f32[256,256]{1,0:T(8,128)S(1)} %shard_map.41), channel_id=1, source_target_pairs={{0,4},{1,5},{2,6},{3,7},{4,0},{5,1},{6,2},{7,3},{8,12},{9,13},{10,... | collective-permute-start | bytes 786440 | tf_op jit(solution)/shard_map/ppermute | solution.py:315
  28.4 16.8 %collective-permute-start.18 = (f32[256,256]{1,0:T(8,128)S(1)}, f32[256,256]{1,0:T(8,128)S(1)}, u32[]{:S(2)}, u32[]{:S(2)}) collective-permute-start(f32[256,256]{1,0:T(8,128)S(1)} %shard_map.45), channel_id=1, source_target_pairs={{0,4},{1,5},{2,6},{3,7},{4,0},{5,1},{6,2},{7,3},{8,12},{9,13},{10,... | collective-permute-start | bytes 786440 | tf_op jit(solution)/shard_map/ppermute | solution.py:315
  32.1 16.6 %collective-permute-start = (f32[512,128]{1,0:T(8,128)S(1)}, f32[512,128]{1,0:T(8,128)S(1)}, u32[]{:S(2)}, u32[]{:S(2)}) collective-permute-start(f32[512,128]{1,0:T(8,128)S(1)} %get-tuple-element.37), channel_id=1, source_target_pairs={{0,1},{1,0},{2,3},{3,2},{4,5},{5,4},{6,7},{7,6},{8,9},{9,8},{10,11... | collective-permute-start | bytes 786440 | tf_op jit(solution)/shard_map/ppermute | solution.py:315
  35.4 13.8 %collective-permute-start.1 = (f32[512,128]{1,0:T(8,128)S(1)}, f32[512,128]{1,0:T(8,128)S(1)}, u32[]{:S(2)}, u32[]{:S(2)}) collective-permute-start(f32[512,128]{1,0:T(8,128)S(1)} %get-tuple-element.38), channel_id=1, source_target_pairs={{0,2},{1,3},{2,0},{3,1},{4,6},{5,7},{6,4},{7,5},{8,10},{9,11},{10,... | collective-permute-start | bytes 786440 | tf_op jit(solution)/shard_map/ppermute | solution.py:315
  41.0 10.7 %collective-permute-start.2 = (f32[512,128]{1,0:T(8,128)S(1)}, f32[512,128]{1,0:T(8,128)S(1)}, u32[]{:S(2)}, u32[]{:S(2)}) collective-permute-start(f32[512,128]{1,0:T(8,128)S(1)} %get-tuple-element.39), channel_id=1, source_target_pairs={{0,3},{1,2},{2,1},{3,0},{4,7},{5,6},{6,5},{7,4},{8,11},{9,10},{10,... | collective-permute-start | bytes 786440 | tf_op jit(solution)/shard_map/ppermute | solution.py:315
  42.9 14.2 %collective-permute-start.17 = (f32[256,256]{1,0:T(8,128)S(1)}, f32[256,256]{1,0:T(8,128)S(1)}, u32[]{:S(2)}, u32[]{:S(2)}) collective-permute-start(f32[256,256]{1,0:T(8,128)S(1)} %shard_map.43), channel_id=1, source_target_pairs={{0,4},{1,5},{2,6},{3,7},{4,0},{5,1},{6,2},{7,3},{8,12},{9,13},{10,... | collective-permute-start | bytes 786440 | tf_op jit(solution)/shard_map/ppermute | solution.py:315
  45.2 15.9 %collective-permute-start.13 = (f32[256,256]{1,0:T(8,128)S(1)}, f32[256,256]{1,0:T(8,128)S(1)}, u32[]{:S(2)}, u32[]{:S(2)}) collective-permute-start(f32[256,256]{1,0:T(8,128)S(1)} %shard_map.42), channel_id=1, source_target_pairs={{0,8},{1,9},{2,10},{3,11},{4,12},{5,13},{6,14},{7,15},{8,0},{9,1},... | collective-permute-start | bytes 786440 | tf_op jit(solution)/shard_map/ppermute | solution.py:315
  48.7 18.9 %collective-permute-start.20 = (f32[256,256]{1,0:T(8,128)S(1)}, f32[256,256]{1,0:T(8,128)S(1)}, u32[]{:S(2)}, u32[]{:S(2)}) collective-permute-start(f32[256,256]{1,0:T(8,128)S(1)} %shard_map.47), channel_id=1, source_target_pairs={{0,4},{1,5},{2,6},{3,7},{4,0},{5,1},{6,2},{7,3},{8,12},{9,13},{10,... | collective-permute-start | bytes 786440 | tf_op jit(solution)/shard_map/ppermute | solution.py:315
  49.2 28.7 %collective-permute-start.19 = (f32[256,256]{1,0:T(8,128)S(1)}, f32[256,256]{1,0:T(8,128)S(1)}, u32[]{:S(2)}, u32[]{:S(2)}) collective-permute-start(f32[256,256]{1,0:T(8,128)S(1)} %shard_map.46), channel_id=1, source_target_pairs={{0,8},{1,9},{2,10},{3,11},{4,12},{5,13},{6,14},{7,15},{8,0},{9,1},... | collective-permute-start | bytes 786440 | tf_op jit(solution)/shard_map/ppermute | solution.py:315
  61.6 27.6 %collective-permute-start.32 = (f32[256,256]{1,0:T(8,128)S(1)}, f32[256,256]{1,0:T(8,128)S(1)}, u32[]{:S(2)}, u32[]{:S(2)}) collective-permute-start(f32[256,256]{1,0:T(8,128)S(1)} %get-tuple-element.54.refs_2_.refs_0_), channel_id=1, source_target_pairs={{0,8},{1,9},{2,10},{3,11},{4,12},{5,13},{6,14},{7,15},{8,0},{9,1},... | collective-permute-start | bytes 786440 | tf_op jit(solution)/shard_map/ppermute | solution.py:315
  78.4 15.2 %collective-permute-start.29 = (f32[256,256]{1,0:T(8,128)S(1)}, f32[256,256]{1,0:T(8,128)S(1)}, u32[]{:S(2)}, u32[]{:S(2)}) collective-permute-start(f32[256,256]{1,0:T(8,128)S(1)} %get-tuple-element.55.refs_3_.refs_0_), channel_id=1, source_target_pairs={{0,8},{1,9},{2,10},{3,11},{4,12},{5,13},{6,14},{7,15},{8,0},{9,1},... | collective-permute-start | bytes 786440 | tf_op jit(solution)/shard_map/ppermute | solution.py:315
  79.1 1.4 %collective-permute-start.21 = (f32[128,256]{1,0:T(8,128)S(1)}, f32[128,256]{1,0:T(8,128)S(1)}, u32[]{:S(2)}, u32[]{:S(2)}) collective-permute-start(f32[128,256]{1,0:T(8,128)S(1)} %get-tuple-element.57), channel_id=1, source_target_pairs={{0,1},{1,0},{2,3},{3,2},{4,5},{5,4},{6,7},{7,6},{8,9},{9,8},{10,11... | collective-permute-start | bytes 393224 | tf_op jit(solution)/shard_map/ppermute | solution.py:315
  80.6 8.6 %collective-permute-start.22 = (f32[64,256]{1,0:T(8,128)S(1)}, f32[64,256]{1,0:T(8,128)S(1)}, u32[]{:S(2)}, u32[]{:S(2)}) collective-permute-start(f32[64,256]{1,0:T(8,128)S(1)} %get-tuple-element.59), channel_id=1, source_target_pairs={{0,2},{1,3},{2,0},{3,1},{4,6},{5,7},{6,4},{7,5},{8,10},{9,11},{10,... | collective-permute-start | bytes 196616 | tf_op jit(solution)/shard_map/ppermute | solution.py:315
  85.0 35.4 %collective-permute-start.34 = (f32[256,256]{1,0:T(8,128)S(1)}, f32[256,256]{1,0:T(8,128)S(1)}, u32[]{:S(2)}, u32[]{:S(2)}) collective-permute-start(f32[256,256]{1,0:T(8,128)S(1)} %get-tuple-element.54.refs_2_.refs_0_), channel_id=1, source_target_pairs={{0,4},{1,5},{2,6},{3,7},{4,0},{5,1},{6,2},{7,3},{8,12},{9,13},{10,... | collective-permute-start | bytes 786440 | tf_op jit(solution)/shard_map/ppermute | solution.py:315
  89.2 31.6 %collective-permute-start.33 = (f32[256,256]{1,0:T(8,128)S(1)}, f32[256,256]{1,0:T(8,128)S(1)}, u32[]{:S(2)}, u32[]{:S(2)}) collective-permute-start(f32[256,256]{1,0:T(8,128)S(1)} %collective-permute-done.32.refs_0_), channel_id=1, source_target_pairs={{0,4},{1,5},{2,6},{3,7},{4,0},{5,1},{6,2},{7,3},{8,12},{9,13},{10,... | collective-permute-start | bytes 786440 | tf_op jit(solution)/shard_map/ppermute | solution.py:315
  89.2 16.9 %collective-permute-start.23 = (f32[64,256]{1,0:T(8,128)S(1)}, f32[64,256]{1,0:T(8,128)S(1)}, u32[]{:S(2)}, u32[]{:S(2)}) collective-permute-start(f32[64,256]{1,0:T(8,128)S(1)} %shard_map.51.refs_0_), channel_id=1, source_target_pairs={{0,4},{1,5},{2,6},{3,7},{4,0},{5,1},{6,2},{7,3},{8,12},{9,13},{10,... | collective-permute-start | bytes 196616 | tf_op jit(solution)/shard_map/ppermute | solution.py:315
  91.3 30.7 %collective-permute-start.31 = (f32[256,256]{1,0:T(8,128)S(1)}, f32[256,256]{1,0:T(8,128)S(1)}, u32[]{:S(2)}, u32[]{:S(2)}) collective-permute-start(f32[256,256]{1,0:T(8,128)S(1)} %get-tuple-element.55.refs_3_.refs_0_), channel_id=1, source_target_pairs={{0,4},{1,5},{2,6},{3,7},{4,0},{5,1},{6,2},{7,3},{8,12},{9,13},{10,... | collective-permute-start | bytes 786440 | tf_op jit(solution)/shard_map/ppermute | solution.py:315
  93.5 28.9 %collective-permute-start.30 = (f32[256,256]{1,0:T(8,128)S(1)}, f32[256,256]{1,0:T(8,128)S(1)}, u32[]{:S(2)}, u32[]{:S(2)}) collective-permute-start(f32[256,256]{1,0:T(8,128)S(1)} %collective-permute-done.29.refs_0_), channel_id=1, source_target_pairs={{0,4},{1,5},{2,6},{3,7},{4,0},{5,1},{6,2},{7,3},{8,12},{9,13},{10,... | collective-permute-start | bytes 786440 | tf_op jit(solution)/shard_map/ppermute | solution.py:315
  106.1 6.8 %collective-permute-start.24 = (f32[64,256]{1,0:T(8,128)S(1)}, f32[64,256]{1,0:T(8,128)S(1)}, u32[]{:S(2)}, u32[]{:S(2)}) collective-permute-start(f32[64,256]{1,0:T(8,128)S(1)} %shard_map.51.refs_0_), channel_id=1, source_target_pairs={{0,8},{1,9},{2,10},{3,11},{4,12},{5,13},{6,14},{7,15},{8,0},{9,1},... | collective-permute-start | bytes 196616 | tf_op jit(solution)/shard_map/ppermute | solution.py:315
  112.9 6.2 %collective-permute-start.25 = (f32[64,256]{1,0:T(8,128)S(1)}, f32[64,256]{1,0:T(8,128)S(1)}, u32[]{:S(2)}, u32[]{:S(2)}) collective-permute-start(f32[64,256]{1,0:T(8,128)S(1)} %shard_map.51.refs_0_), channel_id=1, source_target_pairs={{0,12},{1,13},{2,14},{3,15},{4,8},{5,9},{6,10},{7,11},{8,4},{9,5},... | collective-permute-start | bytes 196616 | tf_op jit(solution)/shard_map/ppermute | solution.py:315
  119.1 4.3 %collective-permute-start.27 = (f32[64,256]{1,0:T(8,128)S(1)}, f32[64,256]{1,0:T(8,128)S(1)}, u32[]{:S(2)}, u32[]{:S(2)}) collective-permute-start(f32[64,256]{1,0:T(8,128)S(1)} %shard_map.52.refs_0_), channel_id=1, source_target_pairs={{0,2},{1,3},{2,0},{3,1},{4,6},{5,7},{6,4},{7,5},{8,10},{9,11},{10,... | collective-permute-start | bytes 196616 | tf_op jit(solution)/shard_map/ppermute | solution.py:315
  122.8 7.0 %collective-permute-start.35 = (f32[256,256]{1,0:T(8,128)S(1)}, f32[256,256]{1,0:T(8,128)S(1)}, u32[]{:S(2)}, u32[]{:S(2)}) collective-permute-start(f32[256,256]{1,0:T(8,128)S(1)} %get-tuple-element.68), channel_id=1, source_target_pairs={{0,1},{1,0},{2,3},{3,2},{4,5},{5,4},{6,7},{7,6},{8,9},{9,8},{10,11... | collective-permute-start | bytes 786440 | tf_op jit(solution)/shard_map/ppermute | solution.py:315
  122.9 1.6 %collective-permute-start.26 = (f32[64,256]{1,0:T(8,128)S(1)}, f32[64,256]{1,0:T(8,128)S(1)}, u32[]{:S(2)}, u32[]{:S(2)}) collective-permute-start(f32[64,256]{1,0:T(8,128)S(1)} %shard_map.52.refs_0_), channel_id=1, source_target_pairs={{0,1},{1,0},{2,3},{3,2},{4,5},{5,4},{6,7},{7,6},{8,9},{9,8},{10,11... | collective-permute-start | bytes 196616 | tf_op jit(solution)/shard_map/ppermute | solution.py:315
  123.4 1.3 collective-permute-start.28
  129.9 6.9 %collective-permute-start.36 = (f32[256,128]{1,0:T(8,128)S(1)}, f32[256,128]{1,0:T(8,128)S(1)}, u32[]{:S(2)}, u32[]{:S(2)}) collective-permute-start(f32[256,128]{1,0:T(8,128)S(1)} %shard_map.66), channel_id=1, source_target_pairs={{0,2},{1,3},{2,0},{3,1},{4,6},{5,7},{6,4},{7,5},{8,10},{9,11},{10,... | collective-permute-start | bytes 393224 | tf_op jit(solution)/shard_map/ppermute | solution.py:315

commit v2 on v1

--- a/solution.py
+++ b/solution.py
@@ -126,33 +126,41 @@
     )(*args)
 
 
-def blocks_of(samples, which, block, me):
-    count = len(which)
+def blocks_of(samples, wanted, block, me, grant):
+    count, half = len(wanted), block // 2
+    rows = [block if h is None else half for _, h in wanted]
 
     def kernel(me_ref, source, *refs):
         outs, done = refs[:count], refs[count]
+        place = me_ref[0]
         copies = []
-        for k, (bits, out) in enumerate(zip(which, outs)):
-            at = pl.multiple_of((me_ref[0] ^ bits) * block, block)
-            copies.append(pltpu.make_async_copy(source.at[pl.ds(at, block), :], out, done.at[k]))
+        for k, ((even, odd), h) in enumerate(wanted):
+            bits = even + (odd - even) * (place & 1)
+            at = pl.multiple_of((place ^ bits) * block + (h or 0) * half, half)
+            part = source.at[pl.ds(at, rows[k]), :]
+            copies.append(pltpu.make_async_copy(part, outs[k], done.at[k]))
         for c in copies:
             c.start()
         for c in copies:
             c.wait()
 
-    shape = jax.ShapeDtypeStruct((block, samples.shape[1]), jnp.float32)
+    cols = samples.shape[1]
     return pl.pallas_call(
         kernel,
-        out_shape=[shape] * count,
+        out_shape=[jax.ShapeDtypeStruct((r, cols), jnp.float32) for r in rows],
         in_specs=[SMEM, pl.BlockSpec(memory_space=pltpu.HBM)],
         out_specs=[VMEM] * count,
         scratch_shapes=[pltpu.SemaphoreType.DMA((count,))],
         cost_estimate=pl.CostEstimate(
-            flops=0, bytes_accessed=8 * count * math.prod(shape.shape), transcendentals=0
+            flops=0, bytes_accessed=8 * sum(rows) * cols, transcendentals=0
         ),
-        compiler_params=pltpu.CompilerParams(vmem_limit_bytes=12 << 20),
+        compiler_params=pltpu.CompilerParams(vmem_limit_bytes=grant << 20),
         name="blocks",
     )(me, samples)
+
+
+def half_of(ref, half, rows):
+    return ref[...] if ref.shape[0] == rows else ref[half * rows : (half + 1) * rows, :]
 
 
 def sketch_of(parts, mixers, half, extra, last=False):
@@ -161,8 +169,7 @@
 
     def kernel(*refs):
         ins = refs[: count + blend + len(extra)]
-        at = slice(half * rows, (half + 1) * rows)
-        left = jnp.concatenate([r[at, :] for r in ins[:count]], 1)
+        left = jnp.concatenate([half_of(r, half, rows) for r in ins[:count]], 1)
         mixer = jnp.concatenate([r[...] for r in ins[count : count + blend]], 0)
         total = split_dot(left, mixer)
         for r in ins[count + blend :]:
@@ -264,8 +271,7 @@
     depth = turned.shape[1]
 
     def kernel(*refs):
-        at = slice(half * depth, (half + 1) * depth)
-        right = jnp.concatenate([r[at, :] for r in refs[1 : 1 + count]], 1)
+        right = jnp.concatenate([half_of(r, half, depth) for r in refs[1 : 1 + count]], 1)
         total = split_dot(refs[0][...], right)
         if previous is not None:
             total = total + refs[1 + count][...]
@@ -308,8 +314,26 @@
     )[0]
 
 
+HALVED = (3, 2, 1, 0)
+
+
+def sends_of(e):
+    if e in HALVED:
+        return ((2, 0), (3, 0), (1, None), (2, 1), (3, 1))
+    return ((2, None), (3, None), (1, None))
+
+
 def make_local(size):
     quads = size // 4
+
+    depth = quads.bit_length() - 1
+    route = [[4 << k for k in range(depth)], [4 << k for k in reversed(range(depth))]]
+
+    def offset(slot, core):
+        return sum(route[core][k] for k in range(depth) if slot >> k & 1)
+
+    def hop(x, k):
+        return lax.ppermute(x, "tm", [(i, i ^ route[i & 1][k]) for i in range(size)])
 
     def swap(x, bit):
         return lax.ppermute(x, "tm", [(i, i ^ bit) for i in range(size)])
@@ -317,13 +341,8 @@
     def total_gram(keep, sent, me):
         keep, send = add_halves(keep, sent, me)
         part = add_all([keep, swap(send, 2)])
-        if quads <= 4:
-            part = add_all([part] + [swap(part, 4 * e) for e in range(1, quads)])
-        else:
-            bit = 4
-            while bit < size:
-                part = add_all([part, swap(part, bit)])
-                bit *= 2
+        for k in range(depth):
+            part = add_all([part, swap(part, 4 << k)])
         other = swap(part, 2)
         return [part, swap(part, 1), other, swap(other, 1)]
 
@@ -336,30 +355,41 @@
         channels, _ = samples.shape
         block = channels // size
 
+        def pieces(wanted, grant):
+            masks = [
+                (tuple(d ^ offset(e, core ^ (d & 1)) for core in (0, 1)), h) for e, d, h in wanted
+            ]
+            return blocks_of(samples, masks, block, me, grant)
+
         order = list(reversed(range(quads)))
         mail = {}
-        sends = [[(order[0], d) for d in (2, 3, 1)], [(e, d) for e in order[1:] for d in (2, 3, 1)]]
-        for wanted in sends:
-            found = blocks_of(samples, [4 * e + d for e, d in wanted], block, me)
-            for (e, d), x in zip(wanted, found):
-                mail[e, d] = swap(x, d)
-        stay = blocks_of(samples, [4 * e for e in range(quads)], block, me)
+        every = [(e, d, h) for e in order for d, h in sends_of(e)]
+        for k, wanted in enumerate((every[:2], every[2:])):
+            if k:
+                wanted += [(e, 0, None) for e in range(quads)]
+            found = pieces(wanted, 50 if k else 60)
+            for (e, d, h), x in zip(wanted, found):
+                mail[e, d, h] = swap(x, d) if d else x
+
+        def part(e, d, h):
+            return mail[e, d, None] if (e, d, None) in mail else mail[e, d, h]
 
         other = swap(test_matrix, 2)
         across = swap(test_matrix, 1)
         diagonal = swap(other, 1)
         mixers = [test_matrix, across, other, diagonal]
 
-        parts = [None] * quads
+        parts = [
+            [[part(e, d, h) for d in range(4)] for h in (0, 1)] for e in range(quads)
+        ]
         inbox = {(e, h): [] for e in range(quads) for h in (0, 1)}
         mine, turned = [None, None], [None, None]
         for e in order:
-            parts[e] = [stay[e]] + [mail[e, d] for d in (1, 2, 3)]
             for h in (0, 1):
-                found = sketch_of(parts[e], mixers, h, inbox[e, h], last=e == 0)
+                found = sketch_of(parts[e][h], mixers, h, inbox[e, h], last=e == 0)
                 if e:
                     step = e & -e
-                    inbox[e - step, h].append(swap(found[0], 4 * step))
+                    inbox[e - step, h].append(hop(found[0], step.bit_length() - 1))
                 else:
                     mine[h], turned[h] = found
 
@@ -369,16 +399,14 @@
         basis = basis_of(mine, inverse, float(channels) ** 0.5)
 
         held = {(0, h): turned[h] for h in (0, 1)}
-        bit = quads // 2
-        while bit >= 1:
+        for k in reversed(range(depth)):
             for e, h in sorted(held):
-                held[e + bit, h] = swap(held[e, h], 4 * bit)
-            bit //= 2
+                held[e + (1 << k), h] = hop(held[e, h], k)
         projected = None
-        sequence = sorted(held, key=lambda k: (k[1], bin(k[0]).count("1"), -k[0]))
+        sequence = sorted(held, key=lambda k: (bin(k[0]).count("1"), -k[0], k[1]))
         for e, h in sequence:
             last = (e, h) == sequence[-1]
-            projected = project(held[e, h], parts[e], h, projected, last)
+            projected = project(held[e, h], parts[e][h], h, projected, last)
             if not last:
                 projected = projected[0]
         first, second, send = projected

time: 138 us -> 133 us (0.964)
  waiting for transfers between devices: 76.6 us -> 64.8 us
  starting transfers between devices: 38.6 us -> 43.7 us
  Pallas kernels: 19.3 us -> 22.9 us
  local copies, waits for them, and re-layouts: 2.19 us -> 0.01 us
    ppermute x37 -> x32, waiting for transfers between devices: 76.6 us -> 44.9 us  [swap(): return lax.ppermute(x, 'tm', [(i, i ^ bit) for i in range(size)])]
    ppermute x0 -> x12, waiting for transfers between devices: none -> 19.9 us  [hop(): lax.ppermute(x, 'tm', [(i, i ^ route[i & 1][k]) for i in range(size)])]
    ppermute x0 -> x12, starting transfers between devices: none -> 18.7 us  [hop(): lax.ppermute(x, 'tm', [(i, i ^ route[i & 1][k]) for i in range(size)])]
    ppermute x37 -> x32, starting transfers between devices: 38.6 us -> 25 us  [swap(): return lax.ppermute(x, 'tm', [(i, i ^ bit) for i in range(size)])]
    pallas_call x3 -> x2, Pallas kernels: 0.46 us -> 4.01 us  [blocks_of(): pl.pallas_call(kernel, out_shape=[jax.ShapeDtypeStruct((r, cols), jnp.flo...]
    unnamed x4 -> x2, local copies, waits for them, and re-layouts: 2.19 us -> 0.01 us
    pallas_call x27 -> x28, Pallas kernels: 18.8 us -> 18.9 us  [call(): pl.pallas_call(kernel, out_shape=shapes, in_specs=[SMEM if a.dtype == jnp...]
  transfers between devices with their start and end apart: 37 -> 44, of which waited for: 21 -> 24; matrix products, arithmetic and copies ran while one was open for 0% -> 0% of each run, Pallas kernels for 13% -> 17%
where the time goes in v2:
time: 133 us; the launch traced here: 132 us
  waiting for transfers between devices  64.8 us (49%)
  starting transfers between devices  43.7 us (33%)
  Pallas kernels  22.9 us (17%)
    ppermute x32, waiting for transfers between devices, swap(): return lax.ppermute(x, 'tm', [(i, i ^ bit) for i in range(size)])  44.9 us
    ppermute x32, starting transfers between devices, swap(): return lax.ppermute(x, 'tm', [(i, i ^ bit) for i in range(size)])  25 us
    ppermute x12, waiting for transfers between devices, hop(): lax.ppermute(x, 'tm', [(i, i ^ route[i & 1][k]) for i in range(size)])  19.9 us
    pallas_call x28, Pallas kernels, call(): pl.pallas_call(kernel, out_shape=shapes, in_specs=[SMEM if a.dtype == jnp...  18.9 us
    ppermute x12, starting transfers between devices, hop(): lax.ppermute(x, 'tm', [(i, i ^ route[i & 1][k]) for i in range(size)])  18.7 us
    pallas_call x2, Pallas kernels, blocks_of(): pl.pallas_call(kernel, out_shape=[jax.ShapeDtypeStruct((r, cols), jnp.flo...  4.01 us
  transfers between devices with their start and end apart: 44, of which 24 were waited for; matrix products, arithmetic and copies ran while one was open for 0% of the time, Pallas kernels for 17%

profile of v2, /device:TPU:0, one launch (start us, length us, event | category | flops | bytes accessed | tf_op | source)
XLA Modules:
  0.0 132.3 jit_solution(3159570371975839220)
XLA Ops:
  0.6 3.1 %collective-permute-start.4 = (f32[128,256]{1,0:T(8,128)}, f32[128,256]{1,0:T(8,128)S(1)}, u32[]{:S(2)}, u32[]{:S(2)}) collective-permute-start(f32[128,256]{1,0:T(8,128)} %refs_4_.15), channel_id=1, source_target_pairs={{0,2},{1,3},{2,0},{3,1},{4,6},{5,7},{6,4},{7,5},{8,10},{9,11},{10,... | collective-permute-start | bytes 393224 | tf_op jit(solution)/shard_map/ppermute | solution.py:339
  3.7 1.7 %blocks.3 = (f32[256,128]{1,0:T(8,128)}, f32[256,128]{1,0:T(8,128)}) custom-call(s32[1]{0:T(128)} %bitcast.me_ref, f32[8192,128]{1,0:T(8,128)} %source.3), custom_call_target="tpu_custom_call" | custom-call | bytes 524288 | tf_op jit(solution)/shard_map/blocks/pallas_call | solution.py:148
  5.6 1.8 %collective-permute-start.11 = (f32[256,128]{1,0:T(8,128)}, f32[256,128]{1,0:T(8,128)S(1)}, u32[]{:S(2)}, u32[]{:S(2)}) collective-permute-start(f32[256,128]{1,0:T(8,128)} %get-tuple-element.55), channel_id=1, source_target_pairs={{0,3},{1,2},{2,1},{3,0},{4,7},{5,6},{6,5},{7,4},{8,11},{9,10},{10,... | collective-permute-start | bytes 393224 | tf_op jit(solution)/shard_map/ppermute | solution.py:339
  7.3 2.3 %blocks.2 = (f32[512,128]{1,0:T(8,128)S(1)}, f32[256,128]{1,0:T(8,128)S(1)}, f32[256,128]{1,0:T(8,128)S(1)}, f32[256,128]{1,0:T(8,128)S(1)}, f32[256,128]{1,0:T(...) custom-call(s32[1]{0:T(128)} %bitcast.me_ref, ...), custom_call_target="tpu_custom_call" | custom-call | bytes 7864320 | tf_op jit(solution)/shard_map/blocks/pallas_call | solution.py:148
  10.2 1.4 %collective-permute-start.8 = (f32[256,128]{1,0:T(8,128)S(1)}, f32[256,128]{1,0:T(8,128)S(1)}, u32[]{:S(2)}, u32[]{:S(2)}) collective-permute-start(f32[256,128]{1,0:T(8,128)S(1)} %get-tuple-element.51), channel_id=1, source_target_pairs={{0,3},{1,2},{2,1},{3,0},{4,7},{5,6},{6,5},{7,4},{8,11},{9,10},{10,... | collective-permute-start | bytes 393224 | tf_op jit(solution)/shard_map/ppermute | solution.py:339
  11.6 0.5 collective-permute-done.10.refs_2_.refs_3_
  12.2 1.8 %collective-permute-done.11.refs_3_.refs_4_ = f32[256,128]{1,0:T(8,128)S(1)} collective-permute-done((f32[256,128]{1,0:T(8,128)}, f32[256,128]{1,0:T(8,128)S(1)}, u32[]{:S(2)}, u32[]{:S(2)}) %collective-permute-start.11) | collective-permute-done | bytes 131104 | tf_op jit(solution)/shard_map/ppermute | solution.py:339
  13.9 0.5 collective-permute-start.16
  14.4 3.3 %collective-permute-done.7.refs_2_.refs_3_ = f32[256,128]{1,0:T(8,128)S(1)} collective-permute-done((f32[256,128]{1,0:T(8,128)S(1)}, f32[256,128]{1,0:T(8,128)S(1)}, u32[]{:S(2)}, u32[]{:S(2)}) %collective-permute-start.7) | collective-permute-done | bytes 131104 | tf_op jit(solution)/shard_map/ppermute | solution.py:339
  17.7 1.9 %collective-permute-done.8.refs_3_.refs_4_ = f32[256,128]{1,0:T(8,128)S(1)} collective-permute-done((f32[256,128]{1,0:T(8,128)S(1)}, f32[256,128]{1,0:T(8,128)S(1)}, u32[]{:S(2)}, u32[]{:S(2)}) %collective-permute-start.8) | collective-permute-done | bytes 131104 | tf_op jit(solution)/shard_map/ppermute | solution.py:339
  19.6 0.7 collective-permute-start.14
  20.3 3.0 %collective-permute-done.15.refs_2_.refs_3_ = f32[256,128]{1,0:T(8,128)S(1)} collective-permute-done((f32[256,128]{1,0:T(8,128)S(1)}, f32[256,128]{1,0:T(8,128)S(1)}, u32[]{:S(2)}, u32[]{:S(2)}) %collective-permute-start.15) | collective-permute-done | bytes 131104 | tf_op jit(solution)/shard_map/ppermute | solution.py:339
  23.4 1.8 %collective-permute-done.16.refs_3_.refs_4_ = f32[256,128]{1,0:T(8,128)S(1)} collective-permute-done((f32[256,128]{1,0:T(8,128)S(1)}, f32[256,128]{1,0:T(8,128)S(1)}, u32[]{:S(2)}, u32[]{:S(2)}) %collective-permute-start.16) | collective-permute-done | bytes 131104 | tf_op jit(solution)/shard_map/ppermute | solution.py:339
  25.2 0.5 collective-permute-start.23
  25.6 1.9 %collective-permute-start.20 = (f32[256,128]{1,0:T(8,128)S(1)}, f32[256,128]{1,0:T(8,128)S(1)}, u32[]{:S(2)}, u32[]{:S(2)}) collective-permute-start(f32[256,128]{1,0:T(8,128)S(1)} %get-tuple-element.63), channel_id=1, source_target_pairs={{0,2},{1,3},{2,0},{3,1},{4,6},{5,7},{6,4},{7,5},{8,10},{9,11},{10,... | collective-permute-start | bytes 393224 | tf_op jit(solution)/shard_map/ppermute | solution.py:339
  27.6 0.4 shard_map.41
  28.0 0.8 collective-permute-done.22.refs_2_.refs_3_
  28.7 1.9 %collective-permute-done.23.refs_3_.refs_4_ = f32[256,128]{1,0:T(8,128)S(1)} collective-permute-done((f32[256,128]{1,0:T(8,128)S(1)}, f32[256,128]{1,0:T(8,128)S(1)}, u32[]{:S(2)}, u32[]{:S(2)}) %collective-permute-start.23) | collective-permute-done | bytes 131104 | tf_op jit(solution)/shard_map/ppermute | solution.py:339
  30.6 1.6 %collective-permute-start.12 = (f32[256,256]{1,0:T(8,128)S(1)}, f32[256,256]{1,0:T(8,128)S(1)}, u32[]{:S(2)}, u32[]{:S(2)}) collective-permute-start(f32[256,256]{1,0:T(8,128)S(1)} %shard_map.41), channel_id=1, source_target_pairs={{0,4},{1,9},{2,6},{3,11},{4,0},{5,13},{6,2},{7,15},{8,12},{9,1},{1... | collective-permute-start | bytes 786440 | tf_op jit(solution)/shard_map/ppermute | solution.py:336
  32.6 2.1 %collective-permute-done.20.refs_2_.refs_3_ = f32[256,128]{1,0:T(8,128)S(1)} collective-permute-done((f32[256,128]{1,0:T(8,128)S(1)}, f32[256,128]{1,0:T(8,128)S(1)}, u32[]{:S(2)}, u32[]{:S(2)}) %collective-permute-start.20) | collective-permute-done | bytes 131104 | tf_op jit(solution)/shard_map/ppermute | solution.py:339
  34.7 1.6 %collective-permute-start.24 = (f32[256,256]{1,0:T(8,128)S(1)}, f32[256,256]{1,0:T(8,128)S(1)}, u32[]{:S(2)}, u32[]{:S(2)}) collective-permute-start(f32[256,256]{1,0:T(8,128)S(1)} %shard_map.45), channel_id=1, source_target_pairs={{0,4},{1,9},{2,6},{3,11},{4,0},{5,13},{6,2},{7,15},{8,12},{9,1},{1... | collective-permute-start | bytes 786440 | tf_op jit(solution)/shard_map/ppermute | solution.py:336
  36.3 0.5 collective-permute-start.26
  36.8 1.5 %collective-permute-start.27 = (f32[256,128]{1,0:T(8,128)S(1)}, f32[256,128]{1,0:T(8,128)S(1)}, u32[]{:S(2)}, u32[]{:S(2)}) collective-permute-start(f32[256,128]{1,0:T(8,128)S(1)} %get-tuple-element.68), channel_id=1, source_target_pairs={{0,3},{1,2},{2,1},{3,0},{4,7},{5,6},{6,5},{7,4},{8,11},{9,10},{10,... | collective-permute-start | bytes 393224 | tf_op jit(solution)/shard_map/ppermute | solution.py:339
  38.7 3.9 %collective-permute-done.26.refs_2_.refs_3_ = f32[256,128]{1,0:T(8,128)S(1)} collective-permute-done((f32[256,128]{1,0:T(8,128)S(1)}, f32[256,128]{1,0:T(8,128)S(1)}, u32[]{:S(2)}, u32[]{:S(2)}) %collective-permute-start.26) | collective-permute-done | bytes 131104 | tf_op jit(solution)/shard_map/ppermute | solution.py:339
  42.7 2.3 %collective-permute-done.27.refs_3_.refs_4_ = f32[256,128]{1,0:T(8,128)S(1)} collective-permute-done((f32[256,128]{1,0:T(8,128)S(1)}, f32[256,128]{1,0:T(8,128)S(1)}, u32[]{:S(2)}, u32[]{:S(2)}) %collective-permute-start.27) | collective-permute-done | bytes 131104 | tf_op jit(solution)/shard_map/ppermute | solution.py:339
  45.1 2.0 %collective-permute-start.17 = (f32[256,256]{1,0:T(8,128)S(1)}, f32[256,256]{1,0:T(8,128)S(1)}, u32[]{:S(2)}, u32[]{:S(2)}) collective-permute-start(f32[256,256]{1,0:T(8,128)S(1)} %shard_map.43), channel_id=1, source_target_pairs={{0,4},{1,9},{2,6},{3,11},{4,0},{5,13},{6,2},{7,15},{8,12},{9,1},{1... | collective-permute-start | bytes 786440 | tf_op jit(solution)/shard_map/ppermute | solution.py:336
  47.1 1.9 %collective-permute-start.2 = (f32[256,128]{1,0:T(8,128)S(1)}, f32[256,128]{1,0:T(8,128)S(1)}, u32[]{:S(2)}, u32[]{:S(2)}) collective-permute-start(f32[256,128]{1,0:T(8,128)S(1)} %get-tuple-element.47), channel_id=1, source_target_pairs={{0,3},{1,2},{2,1},{3,0},{4,7},{5,6},{6,5},{7,4},{8,11},{9,10},{10,... | collective-permute-start | bytes 393224 | tf_op jit(solution)/shard_map/ppermute | solution.py:339
  49.4 0.8 collective-permute-start.13
  50.5 0.4 shard_map.46
  51.2 1.4 %collective-permute-start.28 = (f32[256,256]{1,0:T(8,128)S(1)}, f32[256,256]{1,0:T(8,128)S(1)}, u32[]{:S(2)}, u32[]{:S(2)}) collective-permute-start(f32[256,256]{1,0:T(8,128)S(1)} %shard_map.47), channel_id=1, source_target_pairs={{0,4},{1,9},{2,6},{3,11},{4,0},{5,13},{6,2},{7,15},{8,12},{9,1},{1... | collective-permute-start | bytes 786440 | tf_op jit(solution)/shard_map/ppermute | solution.py:336
  52.6 0.5 collective-permute-done.2.refs_3_.refs_4_
  53.0 2.5 %collective-permute-start.25 = (f32[256,256]{1,0:T(8,128)S(1)}, f32[256,256]{1,0:T(8,128)S(1)}, u32[]{:S(2)}, u32[]{:S(2)}) collective-permute-start(f32[256,256]{1,0:T(8,128)S(1)} %shard_map.46), channel_id=1, source_target_pairs={{0,8},{1,5},{2,10},{3,7},{4,12},{5,1},{6,14},{7,3},{8,0},{9,13},{1... | collective-permute-start | bytes 786440 | tf_op jit(solution)/shard_map/ppermute | solution.py:336
  55.5 1.1 collective-permute-start.18
  56.6 1.2 collective-permute-done.17.refs_9_
  57.8 7.4 %collective-permute-done.13.refs_8_ = f32[256,256]{1,0:T(8,128)S(1)} collective-permute-done((f32[256,256]{1,0:T(8,128)S(1)}, f32[256,256]{1,0:T(8,128)S(1)}, u32[]{:S(2)}, u32[]{:S(2)}) %collective-permute-start.13) | collective-permute-done | bytes 262176 | tf_op jit(solution)/shard_map/ppermute | solution.py:336
  65.2 0.5 shard_map.44
  65.8 3.3 %collective-permute-done.28.refs_9_ = f32[256,256]{1,0:T(8,128)S(1)} collective-permute-done((f32[256,256]{1,0:T(8,128)S(1)}, f32[256,256]{1,0:T(8,128)S(1)}, u32[]{:S(2)}, u32[]{:S(2)}) %collective-permute-start.28) | collective-permute-done | bytes 262176 | tf_op jit(solution)/shard_map/ppermute | solution.py:336
  69.0 1.5 %collective-permute-done.25.refs_8_ = f32[256,256]{1,0:T(8,128)S(1)} collective-permute-done((f32[256,256]{1,0:T(8,128)S(1)}, f32[256,256]{1,0:T(8,128)S(1)}, u32[]{:S(2)}, u32[]{:S(2)}) %collective-permute-start.25) | collective-permute-done | bytes 262176 | tf_op jit(solution)/shard_map/ppermute | solution.py:336
  70.5 0.5 shard_map.48
  71.0 3.4 %collective-permute-start.36 = (f32[256,256]{1,0:T(8,128)S(1)}, f32[256,256]{1,0:T(8,128)S(1)}, u32[]{:S(2)}, u32[]{:S(2)}) collective-permute-start(f32[256,256]{1,0:T(8,128)S(1)} %get-tuple-element.71.refs_3_.refs_0_), channel_id=1, source_target_pairs={{0,8},{1,5},{2,10},{3,7},{4,12},{5,1},{6,14},{7,3},{8,0},{9,13},{1... | collective-permute-start | bytes 786440 | tf_op jit(solution)/shard_map/ppermute | solution.py:336
  74.5 0.7 shard_map.49
  75.2 1.7 %collective-permute-start.41 = (f32[256,256]{1,0:T(8,128)S(1)}, f32[256,256]{1,0:T(8,128)S(1)}, u32[]{:S(2)}, u32[]{:S(2)}) collective-permute-start(f32[256,256]{1,0:T(8,128)S(1)} %get-tuple-element.70.refs_2_.refs_0_), channel_id=1, source_target_pairs={{0,4},{1,9},{2,6},{3,11},{4,0},{5,13},{6,2},{7,15},{8,12},{9,1},{1... | collective-permute-start | bytes 786440 | tf_op jit(solution)/shard_map/ppermute | solution.py:336
  76.9 0.4 collective-permute-start.40
  77.3 2.4 %collective-permute-start.39 = (f32[256,256]{1,0:T(8,128)S(1)}, f32[256,256]{1,0:T(8,128)S(1)}, u32[]{:S(2)}, u32[]{:S(2)}) collective-permute-start(f32[256,256]{1,0:T(8,128)S(1)} %collective-permute-done.38.refs_0_), channel_id=1, source_target_pairs={{0,4},{1,9},{2,6},{3,11},{4,0},{5,13},{6,2},{7,15},{8,12},{9,1},{1... | collective-permute-start | bytes 786440 | tf_op jit(solution)/shard_map/ppermute | solution.py:336
  79.7 6.5 %collective-permute-done.36.refs_0_ = f32[256,256]{1,0:T(8,128)S(1)} collective-permute-done((f32[256,256]{1,0:T(8,128)S(1)}, f32[256,256]{1,0:T(8,128)S(1)}, u32[]{:S(2)}, u32[]{:S(2)}) %collective-permute-start.36) | collective-permute-done | bytes 262176 | tf_op jit(solution)/shard_map/ppermute | solution.py:336
  86.3 0.9 collective-permute-start.37
  87.2 1.6 %collective-permute-start.30 = (f32[64,256]{1,0:T(8,128)S(1)}, f32[64,256]{1,0:T(8,128)S(1)}, u32[]{:S(2)}, u32[]{:S(2)}) collective-permute-start(f32[64,256]{1,0:T(8,128)S(1)} %get-tuple-element.75), channel_id=1, source_target_pairs={{0,2},{1,3},{2,0},{3,1},{4,6},{5,7},{6,4},{7,5},{8,10},{9,11},{10,... | collective-permute-start | bytes 196616 | tf_op jit(solution)/shard_map/ppermute | solution.py:339
  88.8 3.0 %collective-permute-done.30.refs_1_ = f32[64,256]{1,0:T(8,128)S(1)} collective-permute-done((f32[64,256]{1,0:T(8,128)S(1)}, f32[64,256]{1,0:T(8,128)S(1)}, u32[]{:S(2)}, u32[]{:S(2)}) %collective-permute-start.30) | collective-permute-done | bytes 65568 | tf_op jit(solution)/shard_map/ppermute | solution.py:339
  91.8 1.0 collective-permute-start.31
  93.2 13.0 %collective-permute-done.31.refs_1_ = f32[64,256]{1,0:T(8,128)S(1)} collective-permute-done((f32[64,256]{1,0:T(8,128)S(1)}, f32[64,256]{1,0:T(8,128)S(1)}, u32[]{:S(2)}, u32[]{:S(2)}) %collective-permute-start.31) | collective-permute-done | bytes 65568 | tf_op jit(solution)/shard_map/ppermute | solution.py:339
  106.3 2.0 %collective-permute-start.32 = (f32[64,256]{1,0:T(8,128)S(1)}, f32[64,256]{1,0:T(8,128)S(1)}, u32[]{:S(2)}, u32[]{:S(2)}) collective-permute-start(f32[64,256]{1,0:T(8,128)S(1)} %shard_map.52.refs_0_), channel_id=1, source_target_pairs={{0,8},{1,9},{2,10},{3,11},{4,12},{5,13},{6,14},{7,15},{8,0},{9,1},... | collective-permute-start | bytes 196616 | tf_op jit(solution)/shard_map/ppermute | solution.py:339
  109.8 3.1 %collective-permute-done.32.refs_1_ = f32[64,256]{1,0:T(8,128)S(1)} collective-permute-done((f32[64,256]{1,0:T(8,128)S(1)}, f32[64,256]{1,0:T(8,128)S(1)}, u32[]{:S(2)}, u32[]{:S(2)}) %collective-permute-start.32) | collective-permute-done | bytes 65568 | tf_op jit(solution)/shard_map/ppermute | solution.py:339
  112.9 1.9 %collective-permute-start.34 = (f32[64,256]{1,0:T(8,128)S(1)}, f32[64,256]{1,0:T(8,128)S(1)}, u32[]{:S(2)}, u32[]{:S(2)}) collective-permute-start(f32[64,256]{1,0:T(8,128)S(1)} %shard_map.53.refs_0_), channel_id=1, source_target_pairs={{0,2},{1,3},{2,0},{3,1},{4,6},{5,7},{6,4},{7,5},{8,10},{9,11},{10,... | collective-permute-start | bytes 196616 | tf_op jit(solution)/shard_map/ppermute | solution.py:339
  116.1 0.5 collective-permute-start.33
  116.6 0.6 collective-permute-done.34.refs_2_
  117.3 0.5 collective-permute-done.33.refs_1_
  117.7 0.8 collective-permute-done.35.refs_3_
  118.5 2.7 %shard_map.54 = (f32[256,256]{1,0:T(8,128)S(1)}, f32[256,256]{1,0:T(8,128)S(1)}) custom-call(s32[1]{0:T(128)} %bitcast.me_ref, f32[64,256]{1,0:T(8,128)S(1)} %shard_map.53.refs_0_, f32[64,256]{1,0:T(8,128)S(1)} %collective-permute-done.33.refs_1_, f32[64,256]{1,0:T(8,128)S(1)} %collective-permute-done.34.refs_2_, f32[64,256]{1,0:T(8,128)S(1)} %collective-permute-done.35.refs_3_), custom_call_target="tpu_custom_call" | custom-call | flops 1000000000 | bytes 786436 | tf_op jit(solution)/shard_map/pallas_call | solution.py:117
  121.2 2.4 %shard_map.55 = (f32[256,256]{1,0:T(8,128)S(1)}, f32[256,256]{1,0:T(8,128)S(1)}) custom-call(f32[256,256]{1,0:T(8,128)S(1)} %get-tuple-element.76.work_in, f32[256,256]{1,0:T(8,128)S(1)} %get-tuple-element.77.inv_in), custom_call_target="tpu_custom_call", output_to_operand_aliasing={{0}: (0, {}), {1}: (1, {})} | custom-call | flops 1000000000 | bytes 1048576 | tf_op jit(solution)/shard_map/pallas_call | solution.py:117
  123.7 1.9 %collective-permute-start.43 = (f32[256,128]{1,0:T(8,128)S(1)}, f32[256,128]{1,0:T(8,128)S(1)}, u32[]{:S(2)}, u32[]{:S(2)}) collective-permute-start(f32[256,128]{1,0:T(8,128)S(1)} %shard_map.67), channel_id=1, source_target_pairs={{0,2},{1,3},{2,0},{3,1},{4,6},{5,7},{6,4},{7,5},{8,10},{9,11},{10,... | collective-permute-start | bytes 393224 | tf_op jit(solution)/shard_map/ppermute | solution.py:339
  125.6 2.6 %shard_map.56 = (f32[256,256]{1,0:T(8,128)S(1)}, f32[256,256]{1,0:T(8,128)S(1)}) custom-call(f32[256,256]{1,0:T(8,128)S(1)} %get-tuple-element.78.work_in, f32[256,256]{1,0:T(8,128)S(1)} %get-tuple-element.79.inv_in), custom_call_target="tpu_custom_call", output_to_operand_aliasing={{0}: (0, {}), {1}: (1, {})} | custom-call | flops 1000000000 | bytes 1048576 | tf_op jit(solution)/shard_map/pallas_call | solution.py:117
  128.2 2.0 %shard_map.57 = (f32[256,256]{1,0:T(8,128)S(1)}, f32[256,256]{1,0:T(8,128)S(1)}) custom-call(f32[256,256]{1,0:T(8,128)S(1)} %get-tuple-element.80.work_in, f32[256,256]{1,0:T(8,128)S(1)} %get-tuple-element.81.inv_in), custom_call_target="tpu_custom_call", output_to_operand_aliasing={{0}: (0, {}), {1}: (1, {})} | custom-call | flops 1000000000 | bytes 1048576 | tf_op jit(solution)/shard_map/pallas_call | solution.py:117
  130.2 1.2 shard_map.58
  131.4 0.9 shard_map.68
  (56 shorter events, 6.3 us)
Async XLA Ops:
  0.6 9.4 %collective-permute-start.4 = (f32[128,256]{1,0:T(8,128)}, f32[128,256]{1,0:T(8,128)S(1)}, u32[]{:S(2)}, u32[]{:S(2)}) collective-permute-start(f32[128,256]{1,0:T(8,128)} %refs_4_.15), channel_id=1, source_target_pairs={{0,2},{1,3},{2,0},{3,1},{4,6},{5,7},{6,4},{7,5},{8,10},{9,11},{10,... | collective-permute-start | bytes 393224 | tf_op jit(solution)/shard_map/ppermute | solution.py:339
  3.7 6.5 %collective-permute-start.3 = (f32[128,256]{1,0:T(8,128)}, f32[128,256]{1,0:T(8,128)S(1)}, u32[]{:S(2)}, u32[]{:S(2)}) collective-permute-start(f32[128,256]{1,0:T(8,128)} %refs_4_.15), channel_id=1, source_target_pairs={{0,1},{1,0},{2,3},{3,2},{4,5},{5,4},{6,7},{7,6},{8,9},{9,8},{10,11... | collective-permute-start | bytes 393224 | tf_op jit(solution)/shard_map/ppermute | solution.py:339
  3.7 23.9 %copy-start = (f32[128,256]{1,0:T(8,128)S(1)}, f32[128,256]{1,0:T(8,128)}, u32[]{:S(2)}) copy-start(f32[128,256]{1,0:T(8,128)} %refs_4_.15) | copy-start | bytes 393220
  5.4 6.6 %collective-permute-start.10 = (f32[256,128]{1,0:T(8,128)}, f32[256,128]{1,0:T(8,128)S(1)}, u32[]{:S(2)}, u32[]{:S(2)}) collective-permute-start(f32[256,128]{1,0:T(8,128)} %get-tuple-element.54), channel_id=1, source_target_pairs={{0,2},{1,3},{2,0},{3,1},{4,6},{5,7},{6,4},{7,5},{8,10},{9,11},{10,... | collective-permute-start | bytes 393224 | tf_op jit(solution)/shard_map/ppermute | solution.py:339
  5.6 8.4 %collective-permute-start.11 = (f32[256,128]{1,0:T(8,128)}, f32[256,128]{1,0:T(8,128)S(1)}, u32[]{:S(2)}, u32[]{:S(2)}) collective-permute-start(f32[256,128]{1,0:T(8,128)} %get-tuple-element.55), channel_id=1, source_target_pairs={{0,3},{1,2},{2,1},{3,0},{4,7},{5,6},{6,5},{7,4},{8,11},{9,10},{10,... | collective-permute-start | bytes 393224 | tf_op jit(solution)/shard_map/ppermute | solution.py:339
  9.6 16.0 %collective-permute-start.9 = (f32[512,128]{1,0:T(8,128)S(1)}, f32[512,128]{1,0:T(8,128)S(1)}, u32[]{:S(2)}, u32[]{:S(2)}) collective-permute-start(f32[512,128]{1,0:T(8,128)S(1)} %get-tuple-element.53), channel_id=1, source_target_pairs={{0,1},{1,0},{2,3},{3,2},{4,5},{5,4},{6,7},{7,6},{8,9},{9,8},{10,11... | collective-permute-start | bytes 786440 | tf_op jit(solution)/shard_map/ppermute | solution.py:339
  10.0 7.7 %collective-permute-start.7 = (f32[256,128]{1,0:T(8,128)S(1)}, f32[256,128]{1,0:T(8,128)S(1)}, u32[]{:S(2)}, u32[]{:S(2)}) collective-permute-start(f32[256,128]{1,0:T(8,128)S(1)} %get-tuple-element.50), channel_id=1, source_target_pairs={{0,2},{1,3},{2,0},{3,1},{4,6},{5,7},{6,4},{7,5},{8,10},{9,11},{10,... | collective-permute-start | bytes 393224 | tf_op jit(solution)/shard_map/ppermute | solution.py:339
  10.2 9.4 %collective-permute-start.8 = (f32[256,128]{1,0:T(8,128)S(1)}, f32[256,128]{1,0:T(8,128)S(1)}, u32[]{:S(2)}, u32[]{:S(2)}) collective-permute-start(f32[256,128]{1,0:T(8,128)S(1)} %get-tuple-element.51), channel_id=1, source_target_pairs={{0,3},{1,2},{2,1},{3,0},{4,7},{5,6},{6,5},{7,4},{8,11},{9,10},{10,... | collective-permute-start | bytes 393224 | tf_op jit(solution)/shard_map/ppermute | solution.py:339
  12.1 11.2 %collective-permute-start.15 = (f32[256,128]{1,0:T(8,128)S(1)}, f32[256,128]{1,0:T(8,128)S(1)}, u32[]{:S(2)}, u32[]{:S(2)}) collective-permute-start(f32[256,128]{1,0:T(8,128)S(1)} %get-tuple-element.58), channel_id=1, source_target_pairs={{0,2},{1,3},{2,0},{3,1},{4,6},{5,7},{6,4},{7,5},{8,10},{9,11},{10,... | collective-permute-start | bytes 393224 | tf_op jit(solution)/shard_map/ppermute | solution.py:339
  13.9 11.2 %collective-permute-start.16 = (f32[256,128]{1,0:T(8,128)S(1)}, f32[256,128]{1,0:T(8,128)S(1)}, u32[]{:S(2)}, u32[]{:S(2)}) collective-permute-start(f32[256,128]{1,0:T(8,128)S(1)} %get-tuple-element.59), channel_id=1, source_target_pairs={{0,3},{1,2},{2,1},{3,0},{4,7},{5,6},{6,5},{7,4},{8,11},{9,10},{10,... | collective-permute-start | bytes 393224 | tf_op jit(solution)/shard_map/ppermute | solution.py:339
  17.7 9.9 %collective-permute-start.5 = (f32[128,256]{1,0:T(8,128)S(1)}, f32[128,256]{1,0:T(8,128)S(1)}, u32[]{:S(2)}, u32[]{:S(2)}) collective-permute-start(f32[128,256]{1,0:T(8,128)S(1)} %collective-permute-done.4.refs_6_), channel_id=1, source_target_pairs={{0,1},{1,0},{2,3},{3,2},{4,5},{5,4},{6,7},{7,6},{8,9},{9,8},{10,11... | collective-permute-start | bytes 393224 | tf_op jit(solution)/shard_map/ppermute | solution.py:339
  19.6 17.3 %collective-permute-start.14 = (f32[512,128]{1,0:T(8,128)S(1)}, f32[512,128]{1,0:T(8,128)S(1)}, u32[]{:S(2)}, u32[]{:S(2)}) collective-permute-start(f32[512,128]{1,0:T(8,128)S(1)} %get-tuple-element.57), channel_id=1, source_target_pairs={{0,1},{1,0},{2,3},{3,2},{4,5},{5,4},{6,7},{7,6},{8,9},{9,8},{10,11... | collective-permute-start | bytes 786440 | tf_op jit(solution)/shard_map/ppermute | solution.py:339
  23.3 5.4 %collective-permute-start.22 = (f32[256,128]{1,0:T(8,128)S(1)}, f32[256,128]{1,0:T(8,128)S(1)}, u32[]{:S(2)}, u32[]{:S(2)}) collective-permute-start(f32[256,128]{1,0:T(8,128)S(1)} %get-tuple-element.65), channel_id=1, source_target_pairs={{0,2},{1,3},{2,0},{3,1},{4,6},{5,7},{6,4},{7,5},{8,10},{9,11},{10,... | collective-permute-start | bytes 393224 | tf_op jit(solution)/shard_map/ppermute | solution.py:339
  25.2 5.4 %collective-permute-start.23 = (f32[256,128]{1,0:T(8,128)S(1)}, f32[256,128]{1,0:T(8,128)S(1)}, u32[]{:S(2)}, u32[]{:S(2)}) collective-permute-start(f32[256,128]{1,0:T(8,128)S(1)} %get-tuple-element.66), channel_id=1, source_target_pairs={{0,3},{1,2},{2,1},{3,0},{4,7},{5,6},{6,5},{7,4},{8,11},{9,10},{10,... | collective-permute-start | bytes 393224 | tf_op jit(solution)/shard_map/ppermute | solution.py:339
  25.6 9.1 %collective-permute-start.20 = (f32[256,128]{1,0:T(8,128)S(1)}, f32[256,128]{1,0:T(8,128)S(1)}, u32[]{:S(2)}, u32[]{:S(2)}) collective-permute-start(f32[256,128]{1,0:T(8,128)S(1)} %get-tuple-element.63), channel_id=1, source_target_pairs={{0,2},{1,3},{2,0},{3,1},{4,6},{5,7},{6,4},{7,5},{8,10},{9,11},{10,... | collective-permute-start | bytes 393224 | tf_op jit(solution)/shard_map/ppermute | solution.py:339
  27.6 8.7 %collective-permute-start.21 = (f32[256,128]{1,0:T(8,128)S(1)}, f32[256,128]{1,0:T(8,128)S(1)}, u32[]{:S(2)}, u32[]{:S(2)}) collective-permute-start(f32[256,128]{1,0:T(8,128)S(1)} %get-tuple-element.64), channel_id=1, source_target_pairs={{0,3},{1,2},{2,1},{3,0},{4,7},{5,6},{6,5},{7,4},{8,11},{9,10},{10,... | collective-permute-start | bytes 393224 | tf_op jit(solution)/shard_map/ppermute | solution.py:339
  28.7 16.4 %collective-permute-start.6 = (f32[512,128]{1,0:T(8,128)S(1)}, f32[512,128]{1,0:T(8,128)S(1)}, u32[]{:S(2)}, u32[]{:S(2)}) collective-permute-start(f32[512,128]{1,0:T(8,128)S(1)} %get-tuple-element.49), channel_id=1, source_target_pairs={{0,1},{1,0},{2,3},{3,2},{4,5},{5,4},{6,7},{7,6},{8,9},{9,8},{10,11... | collective-permute-start | bytes 786440 | tf_op jit(solution)/shard_map/ppermute | solution.py:339
  30.6 16.5 %collective-permute-start.12 = (f32[256,256]{1,0:T(8,128)S(1)}, f32[256,256]{1,0:T(8,128)S(1)}, u32[]{:S(2)}, u32[]{:S(2)}) collective-permute-start(f32[256,256]{1,0:T(8,128)S(1)} %shard_map.41), channel_id=1, source_target_pairs={{0,4},{1,9},{2,6},{3,11},{4,0},{5,13},{6,2},{7,15},{8,12},{9,1},{1... | collective-permute-start | bytes 786440 | tf_op jit(solution)/shard_map/ppermute | solution.py:336
  34.7 14.7 %collective-permute-start.24 = (f32[256,256]{1,0:T(8,128)S(1)}, f32[256,256]{1,0:T(8,128)S(1)}, u32[]{:S(2)}, u32[]{:S(2)}) collective-permute-start(f32[256,256]{1,0:T(8,128)S(1)} %shard_map.45), channel_id=1, source_target_pairs={{0,4},{1,9},{2,6},{3,11},{4,0},{5,13},{6,2},{7,15},{8,12},{9,1},{1... | collective-permute-start | bytes 786440 | tf_op jit(solution)/shard_map/ppermute | solution.py:336
  36.3 6.4 %collective-permute-start.26 = (f32[256,128]{1,0:T(8,128)S(1)}, f32[256,128]{1,0:T(8,128)S(1)}, u32[]{:S(2)}, u32[]{:S(2)}) collective-permute-start(f32[256,128]{1,0:T(8,128)S(1)} %get-tuple-element.67), channel_id=1, source_target_pairs={{0,2},{1,3},{2,0},{3,1},{4,6},{5,7},{6,4},{7,5},{8,10},{9,11},{10,... | collective-permute-start | bytes 393224 | tf_op jit(solution)/shard_map/ppermute | solution.py:339
  36.8 8.1 %collective-permute-start.27 = (f32[256,128]{1,0:T(8,128)S(1)}, f32[256,128]{1,0:T(8,128)S(1)}, u32[]{:S(2)}, u32[]{:S(2)}) collective-permute-start(f32[256,128]{1,0:T(8,128)S(1)} %get-tuple-element.68), channel_id=1, source_target_pairs={{0,3},{1,2},{2,1},{3,0},{4,7},{5,6},{6,5},{7,4},{8,11},{9,10},{10,... | collective-permute-start | bytes 393224 | tf_op jit(solution)/shard_map/ppermute | solution.py:339
  42.7 12.9 %collective-permute-start = (f32[512,128]{1,0:T(8,128)S(1)}, f32[512,128]{1,0:T(8,128)S(1)}, u32[]{:S(2)}, u32[]{:S(2)}) collective-permute-start(f32[512,128]{1,0:T(8,128)S(1)} %get-tuple-element.45), channel_id=1, source_target_pairs={{0,1},{1,0},{2,3},{3,2},{4,5},{5,4},{6,7},{7,6},{8,9},{9,8},{10,11... | collective-permute-start | bytes 786440 | tf_op jit(solution)/shard_map/ppermute | solution.py:339
  44.9 6.3 %collective-permute-start.1 = (f32[256,128]{1,0:T(8,128)S(1)}, f32[256,128]{1,0:T(8,128)S(1)}, u32[]{:S(2)}, u32[]{:S(2)}) collective-permute-start(f32[256,128]{1,0:T(8,128)S(1)} %get-tuple-element.46), channel_id=1, source_target_pairs={{0,2},{1,3},{2,0},{3,1},{4,6},{5,7},{6,4},{7,5},{8,10},{9,11},{10,... | collective-permute-start | bytes 393224 | tf_op jit(solution)/shard_map/ppermute | solution.py:339
  45.1 12.7 %collective-permute-start.17 = (f32[256,256]{1,0:T(8,128)S(1)}, f32[256,256]{1,0:T(8,128)S(1)}, u32[]{:S(2)}, u32[]{:S(2)}) collective-permute-start(f32[256,256]{1,0:T(8,128)S(1)} %shard_map.43), channel_id=1, source_target_pairs={{0,4},{1,9},{2,6},{3,11},{4,0},{5,13},{6,2},{7,15},{8,12},{9,1},{1... | collective-permute-start | bytes 786440 | tf_op jit(solution)/shard_map/ppermute | solution.py:336
  47.1 6.0 %collective-permute-start.2 = (f32[256,128]{1,0:T(8,128)S(1)}, f32[256,128]{1,0:T(8,128)S(1)}, u32[]{:S(2)}, u32[]{:S(2)}) collective-permute-start(f32[256,128]{1,0:T(8,128)S(1)} %get-tuple-element.47), channel_id=1, source_target_pairs={{0,3},{1,2},{2,1},{3,0},{4,7},{5,6},{6,5},{7,4},{8,11},{9,10},{10,... | collective-permute-start | bytes 393224 | tf_op jit(solution)/shard_map/ppermute | solution.py:339
  49.4 15.8 %collective-permute-start.13 = (f32[256,256]{1,0:T(8,128)S(1)}, f32[256,256]{1,0:T(8,128)S(1)}, u32[]{:S(2)}, u32[]{:S(2)}) collective-permute-start(f32[256,256]{1,0:T(8,128)S(1)} %shard_map.42), channel_id=1, source_target_pairs={{0,8},{1,5},{2,10},{3,7},{4,12},{5,1},{6,14},{7,3},{8,0},{9,13},{1... | collective-permute-start | bytes 786440 | tf_op jit(solution)/shard_map/ppermute | solution.py:336
  51.2 17.8 %collective-permute-start.28 = (f32[256,256]{1,0:T(8,128)S(1)}, f32[256,256]{1,0:T(8,128)S(1)}, u32[]{:S(2)}, u32[]{:S(2)}) collective-permute-start(f32[256,256]{1,0:T(8,128)S(1)} %shard_map.47), channel_id=1, source_target_pairs={{0,4},{1,9},{2,6},{3,11},{4,0},{5,13},{6,2},{7,15},{8,12},{9,1},{1... | collective-permute-start | bytes 786440 | tf_op jit(solution)/shard_map/ppermute | solution.py:336
  53.0 17.5 %collective-permute-start.25 = (f32[256,256]{1,0:T(8,128)S(1)}, f32[256,256]{1,0:T(8,128)S(1)}, u32[]{:S(2)}, u32[]{:S(2)}) collective-permute-start(f32[256,256]{1,0:T(8,128)S(1)} %shard_map.46), channel_id=1, source_target_pairs={{0,8},{1,5},{2,10},{3,7},{4,12},{5,1},{6,14},{7,3},{8,0},{9,13},{1... | collective-permute-start | bytes 786440 | tf_op jit(solution)/shard_map/ppermute | solution.py:336
  55.5 10.2 %collective-permute-start.18 = (f32[256,128]{1,0:T(8,128)S(1)}, f32[256,128]{1,0:T(8,128)S(1)}, u32[]{:S(2)}, u32[]{:S(2)}) collective-permute-start(f32[256,128]{1,0:T(8,128)S(1)} %get-tuple-element.61), channel_id=1, source_target_pairs={{0,2},{1,3},{2,0},{3,1},{4,6},{5,7},{6,4},{7,5},{8,10},{9,11},{10,... | collective-permute-start | bytes 393224 | tf_op jit(solution)/shard_map/ppermute | solution.py:339
  57.8 7.9 %collective-permute-start.19 = (f32[256,128]{1,0:T(8,128)S(1)}, f32[256,128]{1,0:T(8,128)S(1)}, u32[]{:S(2)}, u32[]{:S(2)}) collective-permute-start(f32[256,128]{1,0:T(8,128)S(1)} %get-tuple-element.62), channel_id=1, source_target_pairs={{0,3},{1,2},{2,1},{3,0},{4,7},{5,6},{6,5},{7,4},{8,11},{9,10},{10,... | collective-permute-start | bytes 393224 | tf_op jit(solution)/shard_map/ppermute | solution.py:339
  65.7 11.6 %collective-permute-start.38 = (f32[256,256]{1,0:T(8,128)S(1)}, f32[256,256]{1,0:T(8,128)S(1)}, u32[]{:S(2)}, u32[]{:S(2)}) collective-permute-start(f32[256,256]{1,0:T(8,128)S(1)} %get-tuple-element.70.refs_2_.refs_0_), channel_id=1, source_target_pairs={{0,8},{1,5},{2,10},{3,7},{4,12},{5,1},{6,14},{7,3},{8,0},{9,13},{1... | collective-permute-start | bytes 786440 | tf_op jit(solution)/shard_map/ppermute | solution.py:336
  71.0 15.3 %collective-permute-start.36 = (f32[256,256]{1,0:T(8,128)S(1)}, f32[256,256]{1,0:T(8,128)S(1)}, u32[]{:S(2)}, u32[]{:S(2)}) collective-permute-start(f32[256,256]{1,0:T(8,128)S(1)} %get-tuple-element.71.refs_3_.refs_0_), channel_id=1, source_target_pairs={{0,8},{1,5},{2,10},{3,7},{4,12},{5,1},{6,14},{7,3},{8,0},{9,13},{1... | collective-permute-start | bytes 786440 | tf_op jit(solution)/shard_map/ppermute | solution.py:336
  75.1 12.1 %collective-permute-start.29 = (f32[128,256]{1,0:T(8,128)S(1)}, f32[128,256]{1,0:T(8,128)S(1)}, u32[]{:S(2)}, u32[]{:S(2)}) collective-permute-start(f32[128,256]{1,0:T(8,128)S(1)} %get-tuple-element.73), channel_id=1, source_target_pairs={{0,1},{1,0},{2,3},{3,2},{4,5},{5,4},{6,7},{7,6},{8,9},{9,8},{10,11... | collective-permute-start | bytes 393224 | tf_op jit(solution)/shard_map/ppermute | solution.py:339
  75.2 34.2 %collective-permute-start.41 = (f32[256,256]{1,0:T(8,128)S(1)}, f32[256,256]{1,0:T(8,128)S(1)}, u32[]{:S(2)}, u32[]{:S(2)}) collective-permute-start(f32[256,256]{1,0:T(8,128)S(1)} %get-tuple-element.70.refs_2_.refs_0_), channel_id=1, source_target_pairs={{0,4},{1,9},{2,6},{3,11},{4,0},{5,13},{6,2},{7,15},{8,12},{9,1},{1... | collective-permute-start | bytes 786440 | tf_op jit(solution)/shard_map/ppermute | solution.py:336
  76.9 38.0 %collective-permute-start.40 = (f32[256,256]{1,0:T(8,128)S(1)}, f32[256,256]{1,0:T(8,128)S(1)}, u32[]{:S(2)}, u32[]{:S(2)}) collective-permute-start(f32[256,256]{1,0:T(8,128)S(1)} %get-tuple-element.71.refs_3_.refs_0_), channel_id=1, source_target_pairs={{0,4},{1,9},{2,6},{3,11},{4,0},{5,13},{6,2},{7,15},{8,12},{9,1},{1... | collective-permute-start | bytes 786440 | tf_op jit(solution)/shard_map/ppermute | solution.py:336
  77.3 37.9 %collective-permute-start.39 = (f32[256,256]{1,0:T(8,128)S(1)}, f32[256,256]{1,0:T(8,128)S(1)}, u32[]{:S(2)}, u32[]{:S(2)}) collective-permute-start(f32[256,256]{1,0:T(8,128)S(1)} %collective-permute-done.38.refs_0_), channel_id=1, source_target_pairs={{0,4},{1,9},{2,6},{3,11},{4,0},{5,13},{6,2},{7,15},{8,12},{9,1},{1... | collective-permute-start | bytes 786440 | tf_op jit(solution)/shard_map/ppermute | solution.py:336
  86.3 29.4 %collective-permute-start.37 = (f32[256,256]{1,0:T(8,128)S(1)}, f32[256,256]{1,0:T(8,128)S(1)}, u32[]{:S(2)}, u32[]{:S(2)}) collective-permute-start(f32[256,256]{1,0:T(8,128)S(1)} %collective-permute-done.36.refs_0_), channel_id=1, source_target_pairs={{0,4},{1,9},{2,6},{3,11},{4,0},{5,13},{6,2},{7,15},{8,12},{9,1},{1... | collective-permute-start | bytes 786440 | tf_op jit(solution)/shard_map/ppermute | solution.py:336
  87.2 4.6 %collective-permute-start.30 = (f32[64,256]{1,0:T(8,128)S(1)}, f32[64,256]{1,0:T(8,128)S(1)}, u32[]{:S(2)}, u32[]{:S(2)}) collective-permute-start(f32[64,256]{1,0:T(8,128)S(1)} %get-tuple-element.75), channel_id=1, source_target_pairs={{0,2},{1,3},{2,0},{3,1},{4,6},{5,7},{6,4},{7,5},{8,10},{9,11},{10,... | collective-permute-start | bytes 196616 | tf_op jit(solution)/shard_map/ppermute | solution.py:339
  91.8 14.4 %collective-permute-start.31 = (f32[64,256]{1,0:T(8,128)S(1)}, f32[64,256]{1,0:T(8,128)S(1)}, u32[]{:S(2)}, u32[]{:S(2)}) collective-permute-start(f32[64,256]{1,0:T(8,128)S(1)} %shard_map.51.refs_0_), channel_id=1, source_target_pairs={{0,4},{1,5},{2,6},{3,7},{4,0},{5,1},{6,2},{7,3},{8,12},{9,13},{10,... | collective-permute-start | bytes 196616 | tf_op jit(solution)/shard_map/ppermute | solution.py:339
  106.3 6.6 %collective-permute-start.32 = (f32[64,256]{1,0:T(8,128)S(1)}, f32[64,256]{1,0:T(8,128)S(1)}, u32[]{:S(2)}, u32[]{:S(2)}) collective-permute-start(f32[64,256]{1,0:T(8,128)S(1)} %shard_map.52.refs_0_), channel_id=1, source_target_pairs={{0,8},{1,9},{2,10},{3,11},{4,12},{5,13},{6,14},{7,15},{8,0},{9,1},... | collective-permute-start | bytes 196616 | tf_op jit(solution)/shard_map/ppermute | solution.py:339
  112.9 4.3 %collective-permute-start.34 = (f32[64,256]{1,0:T(8,128)S(1)}, f32[64,256]{1,0:T(8,128)S(1)}, u32[]{:S(2)}, u32[]{:S(2)}) collective-permute-start(f32[64,256]{1,0:T(8,128)S(1)} %shard_map.53.refs_0_), channel_id=1, source_target_pairs={{0,2},{1,3},{2,0},{3,1},{4,6},{5,7},{6,4},{7,5},{8,10},{9,11},{10,... | collective-permute-start | bytes 196616 | tf_op jit(solution)/shard_map/ppermute | solution.py:339
  116.0 7.6 %collective-permute-start.42 = (f32[256,256]{1,0:T(8,128)S(1)}, f32[256,256]{1,0:T(8,128)S(1)}, u32[]{:S(2)}, u32[]{:S(2)}) collective-permute-start(f32[256,256]{1,0:T(8,128)S(1)} %get-tuple-element.84), channel_id=1, source_target_pairs={{0,1},{1,0},{2,3},{3,2},{4,5},{5,4},{6,7},{7,6},{8,9},{9,8},{10,11... | collective-permute-start | bytes 786440 | tf_op jit(solution)/shard_map/ppermute | solution.py:339
  116.1 1.6 %collective-permute-start.33 = (f32[64,256]{1,0:T(8,128)S(1)}, f32[64,256]{1,0:T(8,128)S(1)}, u32[]{:S(2)}, u32[]{:S(2)}) collective-permute-start(f32[64,256]{1,0:T(8,128)S(1)} %shard_map.53.refs_0_), channel_id=1, source_target_pairs={{0,1},{1,0},{2,3},{3,2},{4,5},{5,4},{6,7},{7,6},{8,9},{9,8},{10,11... | collective-permute-start | bytes 196616 | tf_op jit(solution)/shard_map/ppermute | solution.py:339
  117.2 1.3 collective-permute-start.35
  123.7 7.8 %collective-permute-start.43 = (f32[256,128]{1,0:T(8,128)S(1)}, f32[256,128]{1,0:T(8,128)S(1)}, u32[]{:S(2)}, u32[]{:S(2)}) collective-permute-start(f32[256,128]{1,0:T(8,128)S(1)} %shard_map.67), channel_id=1, source_target_pairs={{0,2},{1,3},{2,0},{3,1},{4,6},{5,7},{6,4},{7,5},{8,10},{9,11},{10,... | collective-permute-start | bytes 393224 | tf_op jit(solution)/shard_map/ppermute | solution.py:339
